TPU v7x, 32 devices: a whole 2x2x4 slice. The times are simulated.
32 devices in a mesh: seq: 2 (over x), dp: 16 (over z, y, core).
Axes of the slice: x: 2, y: 2, z: 4, core: 2. Of those that a mesh axis runs over, the one named last changes fastest.
Arguments:
- tokens: bfloat16 [16, 2048, 768], P('dp', 'seq'), may hold values from -6 to 6
- lengths: int32 [16], P('dp'), may hold values from 1024 to 2048, as said below
- w_qkv: bfloat16 [768, 2304], P('dp'), may hold values from -0.21875 to 0.21875
- bias_qv: bfloat16 [1536], P('dp'), may hold values from -3 to 3
- w_out: bfloat16 [768, 768], P('dp'), may hold values from -4 to 4
- bias_out: bfloat16 [768], P('dp'), may hold values from -3 to 3
- w_up: bfloat16 [768, 3072], P('dp'), may hold values from -0.21875 to 0.21875
- bias_up: bfloat16 [3072], P('dp'), may hold values from -3 to 3
- w_down: bfloat16 [3072, 768], P('dp'), may hold values from -0.109375 to 0.109375
- bias_down: bfloat16 [768], P('dp'), may hold values from -3 to 3
- gain_attn: bfloat16 [768], P('dp'), may hold values from 0.099609375 to 1.8984375
- shift_attn: bfloat16 [768], P('dp'), may hold values from -3 to 3
- gain_ffn: bfloat16 [768], P('dp'), may hold values from 0.099609375 to 1.8984375
- shift_ffn: bfloat16 [768], P('dp'), may hold values from -3 to 3
- cotangent: bfloat16 [16, 2048, 768], P('dp', 'seq'), may hold values from -6 to 6
Outputs:
- result: bfloat16 [16, 2048, 768], P('dp', 'seq')
- grad_tokens: float32 [16, 2048, 768], P('dp', 'seq')
- grad_w_qkv: float32 [768, 2304], P('dp')
- grad_bias_qv: float32 [1536], P('dp')
- grad_w_out: float32 [768, 768], P('dp')
- grad_bias_out: float32 [768], P('dp')
- grad_w_up: float32 [768, 3072], P('dp')
- grad_bias_up: float32 [3072], P('dp')
- grad_w_down: float32 [3072, 768], P('dp')
- grad_bias_down: float32 [768], P('dp')
- grad_gain_attn: float32 [768], P('dp')
- grad_shift_attn: float32 [768], P('dp')
- grad_gain_ffn: float32 [768], P('dp')
- grad_shift_ffn: float32 [768], P('dp')
Inputs may be any that keep to these rules, and one draw needn't show every extreme that they name: `lengths`: in every draw some sequence is exactly 2048 long and some other exactly 1024.
All inputs are finite; a program needn't handle non-finite values.
Results may differ from a plain program's by a relative error of at most 0.015.
Values may be sent and summed in bfloat16 or wider, within the bound.
A program may use at most 256 MiB of HBM per device.

v0:
```python
import jax
import jax.numpy as jnp
from jax import lax
from jax.sharding import PartitionSpec as P

HEADS = 12
HD = 64


EPS = 1e-05


def layer_norm(values, gain, offset):
    center = jnp.mean(values, axis=-1, keepdims=True)
    shifted = values - center
    spread = jnp.mean(shifted * shifted, axis=-1, keepdims=True)
    return shifted * lax.rsqrt(spread + EPS) * gain + offset


def gelu_exact(values):
    return 0.5 * values * (1.0 + lax.erf(values * 0.7071067811865476))


def matmul(left, right):
    return jnp.dot(left, right, preferred_element_type=jnp.float32)


def matmul_tn(left, right):
    return lax.dot_general(
        left, right, (((0,), (0,)), ((), ())), preferred_element_type=jnp.float32
    )


def matmul_nt(left, right):
    return lax.dot_general(
        left, right, (((1,), (1,)), ((), ())), preferred_element_type=jnp.float32
    )


def column_sum(values):
    return jnp.sum(values.astype(jnp.float32), axis=0)


def local(
    tokens,
    lengths,
    w_qkv,
    bias_qv,
    w_out,
    bias_out,
    w_up,
    bias_up,
    w_down,
    bias_down,
    gain_attn,
    shift_attn,
    gain_ffn,
    shift_ffn,
    cotangent,
):
    inputs = tokens[0]
    rows_dev = inputs.shape[0]
    width = inputs.shape[1]
    groups = lax.axis_size("seq")
    slot_rows = rows_dev * groups
    head_width = width // groups
    heads_dev = HEADS // groups
    scale = HD ** (-0.5)
    (
        full_qkv,
        full_bqv,
        full_wout,
        full_bout,
        full_wup,
        full_bup,
        full_wdown,
        full_bdown,
        full_gain_one,
        full_shift_one,
        full_gain_two,
        full_shift_two,
    ) = (
        lax.all_gather(w_qkv, "dp", axis=0, tiled=True),
        lax.all_gather(bias_qv, "dp", axis=0, tiled=True),
        lax.all_gather(w_out, "dp", axis=0, tiled=True),
        lax.all_gather(bias_out, "dp", axis=0, tiled=True),
        lax.all_gather(w_up, "dp", axis=0, tiled=True),
        lax.all_gather(bias_up, "dp", axis=0, tiled=True),
        lax.all_gather(w_down, "dp", axis=0, tiled=True),
        lax.all_gather(bias_down, "dp", axis=0, tiled=True),
        lax.all_gather(gain_attn, "dp", axis=0, tiled=True),
        lax.all_gather(shift_attn, "dp", axis=0, tiled=True),
        lax.all_gather(gain_ffn, "dp", axis=0, tiled=True),
        lax.all_gather(shift_ffn, "dp", axis=0, tiled=True),
    )
    gain_first = full_gain_one.astype(jnp.float32)
    shift_first = full_shift_one.astype(jnp.float32)
    gain_second = full_gain_two.astype(jnp.float32)
    shift_second = full_shift_two.astype(jnp.float32)
    projected = matmul(inputs, full_qkv).reshape(rows_dev, 3, width)
    bias_rows = full_bqv.astype(jnp.float32)
    added = jnp.stack([bias_rows[:width], jnp.zeros((width,), jnp.float32), bias_rows[width:]])
    qkv_low = (
        (projected + added[None]).astype(jnp.bfloat16).reshape(rows_dev, 3, groups, head_width)
    )
    regrouped = lax.all_to_all(qkv_low, "seq", split_axis=2, concat_axis=0, tiled=True)
    queries = regrouped[:, 0, 0].reshape(slot_rows, heads_dev, HD)
    keys_all = regrouped[:, 1, 0].reshape(slot_rows, heads_dev, HD)
    values_all = regrouped[:, 2, 0].reshape(slot_rows, heads_dev, HD)
    positions = jnp.arange(slot_rows)
    key_bias = jnp.where(positions < lengths[0], 0.0, -1000000000.0).astype(jnp.float32)
    block_rows = min(512, slot_rows)
    block_count = slot_rows // block_rows
    query_blocks = queries.reshape(block_count, block_rows, heads_dev, HD)

    def score_block(query_block):
        scores = jnp.einsum(
            "qhe,khe->hqk", query_block, keys_all, preferred_element_type=jnp.float32
        )
        return scores * scale + key_bias

    def attend(query_block):
        scores = score_block(query_block)
        largest = jnp.max(scores, axis=-1, keepdims=True)
        exponent = jnp.exp(scores - largest)
        totals = jnp.sum(exponent, axis=-1, keepdims=True)
        weights_soft = exponent / totals
        context = jnp.einsum(
            "hqk,khe->qhe",
            weights_soft.astype(jnp.bfloat16),
            values_all,
            preferred_element_type=jnp.float32,
        )
        return (context.astype(jnp.bfloat16), largest + jnp.log(totals))

    contexts, log_totals = lax.map(attend, query_blocks)
    context_low = contexts.reshape(slot_rows, 1, head_width)
    returned = lax.all_to_all(context_low, "seq", split_axis=0, concat_axis=1, tiled=True).reshape(
        rows_dev, width
    )
    attn_branch = matmul(returned, full_wout) + full_bout.astype(jnp.float32)
    resid_one = inputs.astype(jnp.float32) + attn_branch
    hidden_one, first_pull = jax.vjp(layer_norm, resid_one, gain_first, shift_first)
    hidden_low = hidden_one.astype(jnp.bfloat16)
    pre_act = matmul(hidden_low, full_wup) + full_bup.astype(jnp.float32)
    activated, gelu_pull = jax.vjp(gelu_exact, pre_act)
    act_low = activated.astype(jnp.bfloat16)
    ffn_branch = matmul(act_low, full_wdown) + full_bdown.astype(jnp.float32)
    resid_two = hidden_one + ffn_branch
    output, second_pull = jax.vjp(layer_norm, resid_two, gain_second, shift_second)
    grad_two, grad_gain_two, grad_shift_two = second_pull(cotangent[0].astype(jnp.float32))
    grad_branch = grad_two.astype(jnp.bfloat16)
    grad_wdown = matmul_tn(act_low, grad_branch)
    grad_bdown = column_sum(grad_branch)
    (grad_pre,) = gelu_pull(matmul_nt(grad_branch, full_wdown))
    grad_pre_low = grad_pre.astype(jnp.bfloat16)
    grad_wup = matmul_tn(hidden_low, grad_pre_low)
    grad_bup = column_sum(grad_pre_low)
    grad_hidden = grad_two + matmul_nt(grad_pre_low, full_wup)
    grad_one, grad_gain_one, grad_shift_one = first_pull(grad_hidden)
    grad_proj = grad_one.astype(jnp.bfloat16)
    grad_wout = matmul_tn(returned, grad_proj)
    grad_bout = column_sum(grad_proj)
    grad_context = (
        matmul_nt(grad_proj, full_wout).astype(jnp.bfloat16).reshape(rows_dev, groups, head_width)
    )
    grad_heads = lax.all_to_all(grad_context, "seq", split_axis=1, concat_axis=0, tiled=True)
    grad_blocks = grad_heads.reshape(block_count, block_rows, heads_dev, HD)

    def attend_back(carry, item):
        grad_keys, grad_values = carry
        query_block, grad_block, log_block = item
        weights_soft = jnp.exp(score_block(query_block) - log_block)
        soft_low = weights_soft.astype(jnp.bfloat16)
        grad_values = grad_values + jnp.einsum(
            "hqk,qhe->khe", soft_low, grad_block, preferred_element_type=jnp.float32
        )
        grad_soft = jnp.einsum(
            "qhe,khe->hqk", grad_block, values_all, preferred_element_type=jnp.float32
        )
        inner = jnp.sum(weights_soft * grad_soft, axis=-1, keepdims=True)
        grad_scores = (weights_soft * (grad_soft - inner)).astype(jnp.bfloat16)
        grad_query = (
            jnp.einsum("hqk,khe->qhe", grad_scores, keys_all, preferred_element_type=jnp.float32)
            * scale
        )
        grad_keys = (
            grad_keys
            + jnp.einsum(
                "hqk,qhe->khe", grad_scores, query_block, preferred_element_type=jnp.float32
            )
            * scale
        )
        return ((grad_keys, grad_values), grad_query)

    zeros_grad = jnp.zeros((slot_rows, heads_dev, HD), jnp.float32)
    (grad_keys, grad_values), grad_queries = lax.scan(
        attend_back, (zeros_grad, zeros_grad), (query_blocks, grad_blocks, log_totals)
    )
    grad_stack = jnp.stack(
        [
            grad_queries.reshape(slot_rows, head_width),
            grad_keys.reshape(slot_rows, head_width),
            grad_values.reshape(slot_rows, head_width),
        ],
        axis=1,
    )
    grad_stack = grad_stack.astype(jnp.bfloat16).reshape(slot_rows, 3, 1, head_width)
    grad_qkv = lax.all_to_all(grad_stack, "seq", split_axis=0, concat_axis=2, tiled=True).reshape(
        rows_dev, 3 * width
    )
    grad_wqkv = matmul_tn(inputs, grad_qkv)
    summed_qkv = column_sum(grad_qkv)
    grad_bqv = jnp.concatenate([summed_qkv[:width], summed_qkv[2 * width :]])
    grad_inputs = grad_one + matmul_nt(grad_qkv, full_qkv)
    shares = (
        lax.psum_scatter(grad_wqkv, "dp", scatter_dimension=0, tiled=True),
        lax.psum_scatter(grad_bqv, "dp", scatter_dimension=0, tiled=True),
        lax.psum_scatter(grad_wout, "dp", scatter_dimension=0, tiled=True),
        lax.psum_scatter(grad_bout, "dp", scatter_dimension=0, tiled=True),
        lax.psum_scatter(grad_wup, "dp", scatter_dimension=0, tiled=True),
        lax.psum_scatter(grad_bup, "dp", scatter_dimension=0, tiled=True),
        lax.psum_scatter(grad_wdown, "dp", scatter_dimension=0, tiled=True),
        lax.psum_scatter(grad_bdown, "dp", scatter_dimension=0, tiled=True),
        lax.psum_scatter(grad_gain_one, "dp", scatter_dimension=0, tiled=True),
        lax.psum_scatter(grad_shift_one, "dp", scatter_dimension=0, tiled=True),
        lax.psum_scatter(grad_gain_two, "dp", scatter_dimension=0, tiled=True),
        lax.psum_scatter(grad_shift_two, "dp", scatter_dimension=0, tiled=True),
    )
    (
        share_qkv,
        share_bqv,
        share_wout,
        share_bout,
        share_wup,
        share_bup,
        share_wdown,
        share_bdown,
        share_gain_one,
        share_shift_one,
        share_gain_two,
        share_shift_two,
    ) = shares
    shards = (
        lax.psum(share_qkv.astype(jnp.bfloat16), "seq").astype(jnp.float32),
        lax.psum(share_bqv.astype(jnp.bfloat16), "seq").astype(jnp.float32),
        lax.psum(share_wout.astype(jnp.bfloat16), "seq").astype(jnp.float32),
        lax.psum(share_bout.astype(jnp.bfloat16), "seq").astype(jnp.float32),
        lax.psum(share_wup.astype(jnp.bfloat16), "seq").astype(jnp.float32),
        lax.psum(share_bup.astype(jnp.bfloat16), "seq").astype(jnp.float32),
        lax.psum(share_wdown.astype(jnp.bfloat16), "seq").astype(jnp.float32),
        lax.psum(share_bdown.astype(jnp.bfloat16), "seq").astype(jnp.float32),
        lax.psum(share_gain_one.astype(jnp.bfloat16), "seq").astype(jnp.float32),
        lax.psum(share_shift_one.astype(jnp.bfloat16), "seq").astype(jnp.float32),
        lax.psum(share_gain_two.astype(jnp.bfloat16), "seq").astype(jnp.float32),
        lax.psum(share_shift_two.astype(jnp.bfloat16), "seq").astype(jnp.float32),
    )
    return (output.astype(jnp.bfloat16)[None], grad_inputs[None]) + tuple(shards)


def solution(mesh):
    in_specs = (
        P("dp", "seq", None),
        P("dp"),
        P("dp", None),
        P("dp"),
        P("dp", None),
        P("dp"),
        P("dp", None),
        P("dp"),
        P("dp", None),
        P("dp"),
        P("dp"),
        P("dp"),
        P("dp"),
        P("dp"),
        P("dp", "seq", None),
    )
    out_specs = (
        P("dp", "seq", None),
        P("dp", "seq", None),
        P("dp", None),
        P("dp"),
        P("dp", None),
        P("dp"),
        P("dp", None),
        P("dp"),
        P("dp", None),
        P("dp"),
        P("dp"),
        P("dp"),
        P("dp"),
        P("dp"),
    )
    return jax.shard_map(local, mesh=mesh, in_specs=in_specs, out_specs=out_specs, check_vma=False)
```

profile of v0, /device:TPU:0, one launch (start us, length us, event | category | flops | bytes accessed | tf_op | source)
XLA Modules:
  0.0 1253.0 jit_solution(12332146206228527504)
XLA Ops:
  19.4 63.7 %all-reduce.17 = (bf16[1536]{0:T(1024)(128)(2,1)S(1)}, bf16[768]{0:T(1024)(128)(2,1)}, bf16[768]{0:T(1024)(128)(2,1)}, bf16[768]{0:T(1024)(128)(2,1)}, bf16[3072...) all-reduce(bf16[1536]{0:T(1024)(128)(2,1)S(1)} %dynamic-update-slic, ...), channel_id=1, replica_groups=mesh['seq'=2,'dp'=16] {'dp'}, use_global_device_ids=true, to_apply=%add | all-reduce | flops 9216 | bytes 36864
  107.7 48.3 %all-to-all-done = bf16[1024,3,2,384]{3,0,1,2:T(8,128)(2,1)} async-done(((bf16[1024,3,2,384]{3,0,1,2:T(8,128)(2,1)}), bf16[1024,3,2,384]{3,0,1,2:T(8,128)(2,1)}, u32[]{:S(2)}, u32[]{:S(2)}) %all-to-all-start) | async-done | bytes 4718624 | tf_op jit(solution)/shard_map/all_to_all | solution.py:106
  173.3 106.9 %while.28 = (s32[]{:T(128)}, bf16[4,512,6,64]{1,3,2,0:T(8,128)(2,1)}, f32[4,6,512,1]{2,1,3,0:T(8,128)S(1)}, bf16[4,512,6,64]{1,3,2,0:T(8,128)(2,1)}, bf16[2048,6...) while((s32[]{:T(128)}, bf16[4,512,6,64]{1,3,2,0:T(8,128)(2,1)}, ...), condition=%wide.region_3.4_spmd.clone, body=%wide.region_0.3_spmd.clone.sunk | while | flops 1686307840 | bytes 180237424 | solution.py:136
  188.1 12.5 fusion.115
  214.8 12.4 fusion.115
  241.3 12.4 fusion.115
  267.8 12.4 fusion.115
  298.1 10.8 all-to-all-done.1
  321.1 13.6 %multiply_convert_fusion.1 = (bf16[1024,3072]{1,0:T(8,128)(2,1)}, f32[1024,3072]{1,0:T(8,128)}) fusion(f32[3072]{0:T(1024)S(1)} %convert_element_type.172, bf16[768,3072]{1,0:T(8,128)(2,1)} %all-gather.9.cloned.1.call-done, f32[1024,768]{0,1:T(8,128)} %copy-done.9, f32[768]{0:T(1024)S(1)} %convert_element_type.170, f32[768]{0:T(1024)S(1)} %convert_element_type.169, ...), kind=kOutput, calls=%fused_computation.49 | convolution fusion | flops 4854644736 | bytes 26765312 | tf_op jit(solution)/shard_map/dot_general | solution.py:25
  350.6 15.5 %convert_reduce_fusion = (f32[3072]{0:T(1024)}, bf16[1024,3072]{1,0:T(8,128)(2,1)S(1)}) fusion(bf16[1024,768]{0,1:T(8,128)(2,1)S(1)} %get-tuple-element.403, bf16[3072,768]{1,0:T(8,128)(2,1)S(1)} %bitcast.200, f32[1024,3072]{1,0:T(8,128)} %get-tuple-element.427, f32[3072]{0:T(1024)S(1)} %convert_element_type.172), kind=kOutput, calls=%fused_computation.47 | convolution fusion | flops 4882166784 | bytes 25190400 | tf_op jit(solution)/shard_map/dot_general | solution.py:35
  407.1 328.7 %while.29 = (s32[]{:T(128)}, f32[2048,6,64]{0,2,1:T(8,128)}, f32[2048,6,64]{0,2,1:T(8,128)}, bf16[4,512,6,64]{1,3,2,0:T(8,128)(2,1)}, bf16[4,512,6,64]{1,3,2,0:T...) while((s32[]{:T(128)}, f32[2048,6,64]{0,2,1:T(8,128)}, ...), condition=%wide.region_14.15_spmd.clone, body=%wide.region_12.14_spmd.clone.sunk | while | flops 4125033472 | bytes 208525968 | solution.py:197
  407.5 11.2 fusion.125
  419.4 17.0 %multiply_reduce_fusion.6 = (f32[6,512]{1,0:T(8,128)S(1)}, f32[6,512,2048]{2,1,0:T(8,128)}) fusion(f32[6,512,2048]{2,1,0:T(8,128)} %fusion.125, f32[6,512]{1,0:T(8,128)S(1)} %dynamic-slice_bitcast_fusion.2, f32[2048]{0:T(1024)S(1)} %fusion.126, bf16[2048,6,64]{0,2,1:T(8,128)(2,1)S(1)} %get-tuple-element.601, ...), kind=kOutput, calls=%fused_computation.20.clone.1 | convolution fusion | flops 836760576 | bytes 52331008 | tf_op jit(solution)/shard_map/while/body/eval_jaxpr/qhe,khe->hqk/dot_general | solution.py:178
  436.4 21.6 %multiply_convert_fusion.3 = bf16[6,512,2048]{2,1,0:T(8,128)(2,1)} fusion(f32[6,512,2048]{2,1,0:T(8,128)} %get-tuple-element.543, f32[6,512,2048]{2,1,0:T(8,128)} %fusion.125, f32[6,512]{1,0:T(8,128)S(1)} %get-tuple-element.544, f32[6,512]{1,0:T(8,128)S(1)} %dynamic-slice_bitcast_fusion.2, f32[2048]{0:T(1024)S(1)} %fusion.126), kind=kLoop, calls=%fused_computation.19.clone.1 | loop fusion | flops 37748736 | bytes 62947328 | tf_op jit(solution)/shard_map/while/body/eval_jaxpr/convert_element_type | solution.py:182
  475.9 12.4 bitcast_add_fusion.5
  488.3 11.2 fusion.125
  500.2 16.6 %multiply_reduce_fusion.6 = (f32[6,512]{1,0:T(8,128)S(1)}, f32[6,512,2048]{2,1,0:T(8,128)}) fusion(f32[6,512,2048]{2,1,0:T(8,128)} %fusion.125, f32[6,512]{1,0:T(8,128)S(1)} %dynamic-slice_bitcast_fusion.2, f32[2048]{0:T(1024)S(1)} %fusion.126, bf16[2048,6,64]{0,2,1:T(8,128)(2,1)S(1)} %get-tuple-element.601, ...), kind=kOutput, calls=%fused_computation.20.clone.1 | convolution fusion | flops 836760576 | bytes 52331008 | tf_op jit(solution)/shard_map/while/body/eval_jaxpr/qhe,khe->hqk/dot_general | solution.py:178
  516.7 21.3 %multiply_convert_fusion.3 = bf16[6,512,2048]{2,1,0:T(8,128)(2,1)} fusion(f32[6,512,2048]{2,1,0:T(8,128)} %get-tuple-element.543, f32[6,512,2048]{2,1,0:T(8,128)} %fusion.125, f32[6,512]{1,0:T(8,128)S(1)} %get-tuple-element.544, f32[6,512]{1,0:T(8,128)S(1)} %dynamic-slice_bitcast_fusion.2, f32[2048]{0:T(1024)S(1)} %fusion.126), kind=kLoop, calls=%fused_computation.19.clone.1 | loop fusion | flops 37748736 | bytes 62947328 | tf_op jit(solution)/shard_map/while/body/eval_jaxpr/convert_element_type | solution.py:182
  557.0 13.8 %bitcast_add_fusion.5 = f32[2048,6,64]{0,2,1:T(8,128)} fusion(f32[2048,6,64]{0,2,1:T(8,128)} %get-tuple-element.583, f32[6,512,2048]{2,1,0:T(8,128)} %fusion.125, f32[6,512]{1,0:T(8,128)S(1)} %dynamic-slice_bitcast_fusion.2, f32[2048]{0:T(1024)S(1)} %fusion.126, pred[]{:T(512)S(6)} %compare.3, bf16[4,512,6,64]{1,3,2,0:T(8,128)(2,1)} %get-tuple-element.600, ...), kind=kOutput, calls=%fused_computation.24.clone.1 | convolution fusion | flops 832045056 | bytes 31871488 | tf_op jit(solution)/shard_map/while/body/eval_jaxpr/hqk,qhe->khe/dot_general | solution.py:175
  570.8 11.2 fusion.125
  582.6 16.6 %multiply_reduce_fusion.6 = (f32[6,512]{1,0:T(8,128)S(1)}, f32[6,512,2048]{2,1,0:T(8,128)}) fusion(f32[6,512,2048]{2,1,0:T(8,128)} %fusion.125, f32[6,512]{1,0:T(8,128)S(1)} %dynamic-slice_bitcast_fusion.2, f32[2048]{0:T(1024)S(1)} %fusion.126, bf16[2048,6,64]{0,2,1:T(8,128)(2,1)S(1)} %get-tuple-element.601, ...), kind=kOutput, calls=%fused_computation.20.clone.1 | convolution fusion | flops 836760576 | bytes 52331008 | tf_op jit(solution)/shard_map/while/body/eval_jaxpr/qhe,khe->hqk/dot_general | solution.py:178
  599.2 21.3 %multiply_convert_fusion.3 = bf16[6,512,2048]{2,1,0:T(8,128)(2,1)} fusion(f32[6,512,2048]{2,1,0:T(8,128)} %get-tuple-element.543, f32[6,512,2048]{2,1,0:T(8,128)} %fusion.125, f32[6,512]{1,0:T(8,128)S(1)} %get-tuple-element.544, f32[6,512]{1,0:T(8,128)S(1)} %dynamic-slice_bitcast_fusion.2, f32[2048]{0:T(1024)S(1)} %fusion.126), kind=kLoop, calls=%fused_computation.19.clone.1 | loop fusion | flops 37748736 | bytes 62947328 | tf_op jit(solution)/shard_map/while/body/eval_jaxpr/convert_element_type | solution.py:182
  639.5 13.7 %bitcast_add_fusion.5 = f32[2048,6,64]{0,2,1:T(8,128)} fusion(f32[2048,6,64]{0,2,1:T(8,128)} %get-tuple-element.583, f32[6,512,2048]{2,1,0:T(8,128)} %fusion.125, f32[6,512]{1,0:T(8,128)S(1)} %dynamic-slice_bitcast_fusion.2, f32[2048]{0:T(1024)S(1)} %fusion.126, pred[]{:T(512)S(6)} %compare.3, bf16[4,512,6,64]{1,3,2,0:T(8,128)(2,1)} %get-tuple-element.600, ...), kind=kOutput, calls=%fused_computation.24.clone.1 | convolution fusion | flops 832045056 | bytes 31871488 | tf_op jit(solution)/shard_map/while/body/eval_jaxpr/hqk,qhe->khe/dot_general | solution.py:175
  653.2 11.2 fusion.125
  665.0 16.6 %multiply_reduce_fusion.6 = (f32[6,512]{1,0:T(8,128)S(1)}, f32[6,512,2048]{2,1,0:T(8,128)}) fusion(f32[6,512,2048]{2,1,0:T(8,128)} %fusion.125, f32[6,512]{1,0:T(8,128)S(1)} %dynamic-slice_bitcast_fusion.2, f32[2048]{0:T(1024)S(1)} %fusion.126, bf16[2048,6,64]{0,2,1:T(8,128)(2,1)S(1)} %get-tuple-element.601, ...), kind=kOutput, calls=%fused_computation.20.clone.1 | convolution fusion | flops 836760576 | bytes 52331008 | tf_op jit(solution)/shard_map/while/body/eval_jaxpr/qhe,khe->hqk/dot_general | solution.py:178
  681.6 21.3 %multiply_convert_fusion.3 = bf16[6,512,2048]{2,1,0:T(8,128)(2,1)} fusion(f32[6,512,2048]{2,1,0:T(8,128)} %get-tuple-element.543, f32[6,512,2048]{2,1,0:T(8,128)} %fusion.125, f32[6,512]{1,0:T(8,128)S(1)} %get-tuple-element.544, f32[6,512]{1,0:T(8,128)S(1)} %dynamic-slice_bitcast_fusion.2, f32[2048]{0:T(1024)S(1)} %fusion.126), kind=kLoop, calls=%fused_computation.19.clone.1 | loop fusion | flops 37748736 | bytes 62947328 | tf_op jit(solution)/shard_map/while/body/eval_jaxpr/convert_element_type | solution.py:182
  721.9 13.8 %bitcast_add_fusion.5 = f32[2048,6,64]{0,2,1:T(8,128)} fusion(f32[2048,6,64]{0,2,1:T(8,128)} %get-tuple-element.583, f32[6,512,2048]{2,1,0:T(8,128)} %fusion.125, f32[6,512]{1,0:T(8,128)S(1)} %dynamic-slice_bitcast_fusion.2, f32[2048]{0:T(1024)S(1)} %fusion.126, pred[]{:T(512)S(6)} %compare.3, bf16[4,512,6,64]{1,3,2,0:T(8,128)(2,1)} %get-tuple-element.600, ...), kind=kOutput, calls=%fused_computation.24.clone.1 | convolution fusion | flops 832045056 | bytes 31871488 | tf_op jit(solution)/shard_map/while/body/eval_jaxpr/hqk,qhe->khe/dot_general | solution.py:175
  758.8 67.8 %all_to_all.63 = bf16[2048,3,1,384]{3,1,2,0:T(4,128)(2,1)S(1)} all-to-all(bf16[2048,3,1,384]{3,1,2,0:T(4,128)(2,1)} %copy.150), channel_id=1, replica_groups=mesh['seq'=2,'dp'=16] {'seq'}, dimensions={0} | all-to-all | bytes 9437184 | tf_op jit(solution)/shard_map/all_to_all | solution.py:209
  884.2 78.9 %all-reduce.16 = (bf16[1536]{0:T(1024)(128)(2,1)S(1)}, bf16[768]{0:T(1024)(128)(2,1)S(1)}, bf16[3072]{0:T(1024)(128)(2,1)S(1)}, bf16[768]{0:T(1024)(128)(2,1)S(1...) all-reduce(f32[1536]{0:T(1024)S(1)} %pad_maximum_fusion.2, ...), channel_id=3, replica_groups=mesh['seq'=2,'dp'=16] {'dp'}, use_global_device_ids=true, to_apply=%region_18.19.clone | all-reduce | flops 9216 | bytes 55296
  976.7 98.0 %reduce-scatter.9.cloned.1.call-done = f32[48,3072]{1,0:T(8,128)} async-done(((f32[768,3072]{1,0:T(8,128)}), f32[48,3072]{1,0:T(8,128)}) %reduce-scatter.9.cloned.1.call-update) | async-done | bytes 589840 | tf_op jit(solution)/shard_map/reduce_scatter | solution.py:221
  1076.5 114.0 %reduce-scatter.11.cloned.1.call-done = f32[192,768]{1,0:T(8,128)} async-done(((f32[3072,768]{1,0:T(8,128)}), f32[192,768]{1,0:T(8,128)}) %reduce-scatter.11.cloned.1.call-update) | async-done | bytes 589840 | tf_op jit(solution)/shard_map/reduce_scatter | solution.py:223
  1204.7 34.3 %all-reduce.22.cloned.1.call-done = (bf16[48,2304]{0,1:T(8,128)(2,1)}, bf16[48,768]{1,0:T(8,128)(2,1)}, bf16[48,3072]{1,0:T(8,128)(2,1)}, bf16[192,768]{1,0:T(8,128)(2,1)}) async-done(((bf16[48,2304]{0,1:T(8,128)(2,1)}, bf16[48,768]{1,0:T(8,128)(2,1)}, bf16[48,3072]{1,0:T(8,128)(2,1)}, bf16[192,768]{1,0:T(8,128)(2,1)}), (bf16[48,2304]{0,1:T(8,128)(2,1)}, bf16[48,768]{1,0:T(8,128)(2,1)}, ...) | async-done | bytes 884752 | tf_op jit(solution)/shard_map/psum | solution.py:245
  (288 shorter events, 387.8 us)
Async XLA Ops:
  7.2 76.1 %all-gather.5.cloned.1.call-start = ((), (), s32[]{:S(2)}) async-start(), calls=%async_computation.8 | async-start | bytes 3760128 | tf_op jit(solution)/shard_map/all_gather | solution.py:83
  7.9 307.2 %all-gather.7.cloned.1.call-start = ((), (), s32[]{:S(2)}) async-start(), calls=%async_computation.9 | async-start | bytes 1253376 | tf_op jit(solution)/shard_map/all_gather | solution.py:85
  8.7 312.5 %all-gather.9.cloned.1.call-start = ((), (), s32[]{:S(2)}) async-start(), calls=%async_computation.10 | async-start | bytes 5013504 | tf_op jit(solution)/shard_map/all_gather | solution.py:87
  101.3 54.7 %all-to-all-start = ((bf16[1024,3,2,384]{3,0,1,2:T(8,128)(2,1)}), bf16[1024,3,2,384]{3,0,1,2:T(8,128)(2,1)}, u32[]{:S(2)}, u32[]{:S(2)}) async-start(bf16[1024,3,2,384]{3,0,1,2:T(8,128)(2,1)} %copy.135), calls=%async_computation | async-start | bytes 9437184 | tf_op jit(solution)/shard_map/all_to_all | solution.py:106
  107.1 227.6 %all-gather.11.cloned.1.call-start = ((), (), s32[]{:S(2)}) async-start(), calls=%async_computation.11 | async-start | bytes 5013504 | tf_op jit(solution)/shard_map/all_gather | solution.py:89
  179.1 8.9 copy-start
  206.4 8.4 copy-start
  233.0 8.3 copy-start
  259.5 8.3 copy-start
  290.3 18.5 %all-to-all-start.1 = ((bf16[2,2,196608]{2,1,0:T(2,128)(2,1)}), bf16[2,2,196608]{2,1,0:T(2,128)(2,1)S(1)}, u32[]{:S(2)}, u32[]{:S(2)}) async-start(bf16[2,2,196608]{2,1,0:T(2,128)(2,1)} %reshape.258), calls=%async_computation.1 | async-start | bytes 3145728 | tf_op jit(solution)/shard_map/all_to_all | solution.py:138
  296.2 77.1 %copy-start.24 = (f32[768]{0:T(1024)}, f32[768]{0:T(1024)S(1)}, u32[]{:S(2)}) copy-start(f32[768]{0:T(1024)S(1)} %convert_element_type.169) | copy-start | bytes 9220
  296.3 38.4 %copy-start.33 = (f32[768]{0:T(1024)}, f32[768]{0:T(1024)S(1)}, u32[]{:S(2)}) copy-start(f32[768]{0:T(1024)S(1)} %convert_element_type.170) | copy-start | bytes 9220
  298.1 68.0 %copy-start.5 = (bf16[1,1024,768]{1,2,0:T(8,128)(2,1)}, bf16[1,1024,768]{1,2,0:T(8,128)(2,1)S(1)}, u32[]{:S(2)}) copy-start(bf16[1,1024,768]{1,2,0:T(8,128)(2,1)S(1)} %copy.144) | copy-start | bytes 4718596
  319.0 54.3 %copy-start.20 = (f32[1024]{0:T(1024)}, f32[1024]{0:T(1024)S(1)}, u32[]{:S(2)}) copy-start(f32[1024]{0:T(1024)S(1)} %broadcast_multiply_fusion.1) | copy-start | bytes 12292
  321.1 52.2 %copy-start.26 = (f32[1024]{0:T(1024)}, f32[1024]{0:T(1024)S(1)}, u32[]{:S(2)}) copy-start(f32[1024]{0:T(1024)S(1)} %fusion.49) | copy-start | bytes 12292
  347.2 18.9 %slice-start = ((s8[4718592]{0:T(1024)(128)(4,1)}), s8[4194304]{0:T(1024)(128)(4,1)S(1)}, s32[]{:S(2)}) async-start(s8[4718592]{0:T(1024)(128)(4,1)} %bitcast.197), calls=%async_computation.17 | async-start | bytes 8388608
  350.5 15.6 %copy-start.17 = (bf16[1024,768]{0,1:T(8,128)(2,1)}, bf16[1024,768]{0,1:T(8,128)(2,1)S(1)}, u32[]{:S(2)}) copy-start(bf16[1024,768]{0,1:T(8,128)(2,1)S(1)} %get-tuple-element.403) | copy-start | bytes 4718596
  350.5 15.6 %copy-start.10 = (f32[1024,768]{0,1:T(8,128)S(1)}, f32[1024,768]{0,1:T(8,128)}, u32[]{:S(2)}) copy-start(f32[1024,768]{0,1:T(8,128)} %copy-done.9) | copy-start | bytes 9437188
  350.5 15.6 %slice-start.1 = ((s8[4718592]{0:T(1024)(128)(4,1)}), s8[524288]{0:T(1024)(128)(4,1)S(1)}, s32[]{:S(2)}) async-start(s8[4718592]{0:T(1024)(128)(4,1)} %bitcast.197), calls=%async_computation.18 | async-start | bytes 1048576
  366.1 7.2 copy-start.44
  378.9 17.2 %all-to-all-start.2 = ((bf16[1024,2,384]{0,2,1:T(8,128)(2,1)}), bf16[1024,2,384]{0,2,1:T(8,128)(2,1)S(1)}, u32[]{:S(2)}, u32[]{:S(2)}) async-start(bf16[1024,2,384]{0,2,1:T(8,128)(2,1)} %bitcast.196), calls=%async_computation.2 | async-start | bytes 3145728 | tf_op jit(solution)/shard_map/all_to_all | solution.py:167
  382.7 590.4 %reduce-scatter.7.cloned.1.call-start = ((), (), s32[]{:S(2)}) async-start(), calls=%async_computation.12 | async-start | bytes 2506752 | tf_op jit(solution)/shard_map/reduce_scatter | solution.py:219
  387.0 587.6 %reduce-scatter.13.cloned.1.call-start = ((), (), s32[]{:S(2)}) async-start(), calls=%async_computation.15 | async-start | bytes 7520256
  398.8 8.3 copy-start.1
  398.8 8.3 copy-start.4
  735.8 7.8 copy-start.2
  829.3 6.8 copy-start.15
  852.2 222.5 %reduce-scatter.9.cloned.1.call-start = ((), (), s32[]{:S(2)}) async-start(), calls=%async_computation.13 | async-start | bytes 10027008 | tf_op jit(solution)/shard_map/reduce_scatter | solution.py:221
  864.6 325.9 %reduce-scatter.11.cloned.1.call-start = ((), (), s32[]{:S(2)}) async-start(), calls=%async_computation.14 | async-start | bytes 10027008 | tf_op jit(solution)/shard_map/reduce_scatter | solution.py:223
  876.2 362.8 %all-reduce.22.cloned.1.call-start = ((), (), s32[]{:S(2)}) async-start(), calls=%async_computation.16 | async-start | bytes 2506752 | tf_op jit(solution)/shard_map/psum | solution.py:245
  884.1 308.3 %copy-start.8 = (f32[1024,768]{0,1:T(8,128)S(1)}, f32[1024,768]{0,1:T(8,128)}, u32[]{:S(2)}) copy-start(f32[1024,768]{0,1:T(8,128)} %copy-done.7) | copy-start | bytes 9437188
  884.1 308.3 %copy-start.23 = (f32[1024]{0:T(1024)S(1)}, f32[1024]{0:T(1024)}, u32[]{:S(2)}) copy-start(f32[1024]{0:T(1024)} %copy-done.22) | copy-start | bytes 12292
  (32 other events, 118.1 us)
Sparse Core Ops, SparseCore 0:
  10.3 50.6 all-gather.4
  63.2 36.8 all-gather.6
  102.4 52.3 all-gather.8
  156.9 51.7 all-gather.10
  387.2 68.0 reduce-scatter.6
  852.3 106.9 reduce-scatter.12
  963.4 111.2 reduce-scatter.8
  1079.3 111.1 reduce-scatter.10
  1194.1 44.8 all-reduce.21
where the time goes:
time: 1260 us; the launch traced here: 1250 us
  matrix products  411 us (33%)
  waiting for transfers between devices  317 us (25%)
  blocking collectives  216 us (17%)
  other arithmetic  145 us (12%)
  local copies, waits for them, and re-layouts  130 us (10%)
  between operations  19.2 us (2%)
  starting transfers between devices  14.4 us (1%)
    unnamed x2, blocking collectives  143 us
    reduce_scatter x1, waiting for transfers between devices, local(): lax.psum_scatter(grad_wdown, 'dp', scatter_dimension=0, tiled=True)  114 us
    reduce_scatter x1, waiting for transfers between devices, local(): lax.psum_scatter(grad_wup, 'dp', scatter_dimension=0, tiled=True)  98 us
    convert_element_type x4, other arithmetic, attend_back(): grad_scores = (weights_soft * (grad_soft - inner)).astype(jnp.bfloat16)  85.6 us
    all_to_all x1, blocking collectives, local(): lax.all_to_all(grad_stack, 'seq', split_axis=0, concat_axis=2, tiled=True)  67.8 us
    dot_general x4, matrix products, attend_back(): jnp.einsum('qhe,khe->hqk', grad_block, values_all, preferred_element_type...  66.7 us
    dot_general x8, matrix products, score_block(): jnp.einsum('qhe,khe->hqk', query_block, keys_all, preferred_element_type=...  65.5 us
    dot_general x4, matrix products, attend_back(): jnp.einsum('hqk,qhe->khe', soft_low, grad_block, preferred_element_type=j...  53.7 us
  transfers between devices with their start and end apart: 12, of which 6 were waited for; matrix products, arithmetic and copies ran while one was open for 49% of the time, Pallas kernels for 0%

commit v1 on v0

v1 whole, which is shorter than its diff:
```python
import functools

import jax
import jax.numpy as jnp
from jax import lax
from jax.experimental import pallas as pl
from jax.experimental.pallas import tpu as pltpu
from jax.sharding import PartitionSpec as P

HEADS = 12
HD = 64
EPS = 1e-05
BF = jnp.bfloat16
F32 = jnp.float32
SCALE = HD**-0.5
EXP2_SCALE = SCALE * 1.4426950408889634
MASK = -8e9


def dot_nn(a, b):
    return lax.dot_general(a, b, (((1,), (0,)), ((), ())), preferred_element_type=F32)


def dot_nt(a, b):
    return lax.dot_general(a, b, (((1,), (1,)), ((), ())), preferred_element_type=F32)


def dot_tn(a, b):
    return lax.dot_general(a, b, (((0,), (0,)), ((), ())), preferred_element_type=F32)


def layer_norm(values, gain, offset):
    center = jnp.mean(values, axis=-1, keepdims=True)
    shifted = values - center
    spread = jnp.mean(shifted * shifted, axis=-1, keepdims=True)
    return shifted * lax.rsqrt(spread + EPS) * gain + offset


def gelu_exact(values):
    return 0.5 * values * (1.0 + lax.erf(values * 0.7071067811865476))


def column_sum(values):
    return jnp.sum(values.astype(F32), axis=0)


def attend_kernel(chunk, k_ref, qt_ref, vt_ref, aug_ref, o_ref, lse_ref, *scratch):
    keys = k_ref.shape[0]
    queries = qt_ref.shape[1]
    qt = qt_ref[...]
    row = lax.broadcasted_iota(jnp.int32, (128, queries), 0)
    tail = jnp.where(row == 0, 1.0, 0.0).astype(BF)
    for h in range(2):
        held = scratch[h]
        mine = jnp.where((row >= HD * h) & (row < HD * h + HD), qt, 0).astype(BF)
        query = jnp.concatenate([mine, tail], axis=0)
        largest = jnp.full((1, queries), -jnp.inf, F32)
        for c in range(keys // chunk):
            part = slice(c * chunk, (c + 1) * chunk)
            key = jnp.concatenate([k_ref[part, :], aug_ref[part, :]], axis=1)
            scores = dot_nn(key, query)
            held[part, :] = scores
            largest = jnp.maximum(largest, jnp.max(scores, axis=0, keepdims=True))
        total = jnp.zeros((1, queries), F32)
        context = jnp.zeros((HD, queries), F32)
        base = largest * EXP2_SCALE
        for c in range(keys // chunk):
            part = slice(c * chunk, (c + 1) * chunk)
            weight = jnp.exp2(held[part, :] * EXP2_SCALE - base)
            total = total + jnp.sum(weight, axis=0, keepdims=True)
            context = context + dot_nn(vt_ref[HD * h : HD * h + HD, part], weight.astype(BF))
        o_ref[HD * h : HD * h + HD, :] = (context / total).astype(BF)
        lse_ref[h : h + 1, :] = largest * SCALE + jnp.log(total)


def attend(k, qt, vt, aug):
    keys, width = k.shape
    queries = qt.shape[1]
    pairs = width // 128
    block = min(1024, queries)
    chunk = min(256, keys)
    return pl.pallas_call(
        functools.partial(attend_kernel, chunk),
        grid=(pairs, queries // block),
        in_specs=[
            pl.BlockSpec((keys, 128), lambda g, i: (0, g)),
            pl.BlockSpec((128, block), lambda g, i: (g, i)),
            pl.BlockSpec((128, keys), lambda g, i: (g, 0)),
            pl.BlockSpec((keys, 128), lambda g, i: (0, 0)),
        ],
        out_specs=[
            pl.BlockSpec((128, block), lambda g, i: (g, i)),
            pl.BlockSpec((None, 2, block), lambda g, i: (g, 0, i)),
        ],
        out_shape=[
            jax.ShapeDtypeStruct((width, queries), BF),
            jax.ShapeDtypeStruct((pairs, 2, queries), F32),
        ],
        scratch_shapes=[pltpu.VMEM((keys, block), F32)] * 2,
        compiler_params=pltpu.CompilerParams(vmem_limit_bytes=56 << 20),
        cost_estimate=pl.CostEstimate(
            flops=16 * queries * keys * width, transcendentals=queries * keys * 2 * pairs, bytes_accessed=2 * width * (queries + 2 * keys)
        ),
        name="attend",
    )(k, qt, vt, aug)


def three_terms(row, values):
    high = values.astype(BF).astype(F32)
    middle = (values - high).astype(BF).astype(F32)
    low = values - high - middle
    return jnp.where(row == 1, high, 0.0) + jnp.where(row == 2, middle, 0.0) + jnp.where(row == 3, low, 0.0)


def attend_back_kernel(
    chunk, k_ref, kt_ref, v_ref, qt_ref, q_ref, gt_ref, g_ref, aug_ref, lse_ref, delta_ref, dqt_ref, dk_ref, dv_ref, dk_sum, dv_sum
):
    step = pl.program_id(1)
    keys = k_ref.shape[0]
    queries = qt_ref.shape[1]

    @pl.when(step == 0)
    def _():
        dk_sum[...] = jnp.zeros_like(dk_sum)
        dv_sum[...] = jnp.zeros_like(dv_sum)

    qt = qt_ref[...]
    gt = gt_ref[...]
    q = q_ref[...]
    g = g_ref[...]
    row = lax.broadcasted_iota(jnp.int32, (128, queries), 0)
    lane = lax.broadcasted_iota(jnp.int32, (queries, 128), 1)
    query_cols, grad_cols, query_rows, grad_rows = [], [], [], []
    for h in range(2):
        down = (row >= HD * h) & (row < HD * h + HD)
        across = (lane >= HD * h) & (lane < HD * h + HD)
        tail = three_terms(row, lse_ref[h : h + 1, :] * (1.0 / SCALE)) + jnp.where(row == 0, 1.0, 0.0)
        query_cols.append(jnp.concatenate([jnp.where(down, qt, 0).astype(BF), tail.astype(BF)], axis=0))
        tail = three_terms(row, delta_ref[h : h + 1, :])
        grad_cols.append(jnp.concatenate([jnp.where(down, gt, 0).astype(BF), tail.astype(BF)], axis=0))
        query_rows.append(jnp.where(across, q, 0).astype(BF))
        grad_rows.append(jnp.where(across, g, 0).astype(BF))
    query_rows = jnp.concatenate(query_rows, axis=0)
    grad_rows = jnp.concatenate(grad_rows, axis=0)
    dq = [jnp.zeros((HD, queries), F32)] * 2
    for c in range(keys // chunk):
        part = slice(c * chunk, (c + 1) * chunk)
        aug = aug_ref[part, :]
        key = jnp.concatenate([k_ref[part, :], aug], axis=1)
        value = jnp.concatenate([v_ref[part, :], aug], axis=1)
        weights, grads = [], []
        for h in range(2):
            weight = jnp.exp2(dot_nn(key, query_cols[h]) * EXP2_SCALE)
            grad = (weight * dot_nn(value, grad_cols[h])).astype(BF)
            weights.append(weight.astype(BF))
            grads.append(grad)
            dq[h] = dq[h] + dot_nn(kt_ref[HD * h : HD * h + HD, part], grad)
        dv_sum[part, :] += dot_nn(jnp.concatenate(weights, axis=1), grad_rows)
        dk_sum[part, :] += dot_nn(jnp.concatenate(grads, axis=1), query_rows)
    for h in range(2):
        dqt_ref[HD * h : HD * h + HD, :] = (dq[h] * SCALE).astype(BF)

    @pl.when(step == pl.num_programs(1) - 1)
    def _():
        dk_ref[...] = (dk_sum[...] * SCALE).astype(BF)
        dv_ref[...] = dv_sum[...].astype(BF)


def attend_back(k, kt, v, qt, q, gt, g, aug, lse, delta):
    keys, width = k.shape
    queries = qt.shape[1]
    pairs = width // 128
    block = min(1024, queries)
    chunk = min(256, keys)
    key_rows = pl.BlockSpec((keys, 128), lambda g, i: (0, g))
    query_cols = pl.BlockSpec((128, block), lambda g, i: (g, i))
    query_rows = pl.BlockSpec((block, 128), lambda g, i: (i, g))
    stats = pl.BlockSpec((None, 2, block), lambda g, i: (g, 0, i))
    return pl.pallas_call(
        functools.partial(attend_back_kernel, chunk),
        grid=(pairs, queries // block),
        in_specs=[
            key_rows,
            pl.BlockSpec((128, keys), lambda g, i: (g, 0)),
            key_rows,
            query_cols,
            query_rows,
            query_cols,
            query_rows,
            pl.BlockSpec((keys, 128), lambda g, i: (0, 0)),
            stats,
            stats,
        ],
        out_specs=[query_cols, key_rows, key_rows],
        out_shape=[
            jax.ShapeDtypeStruct((width, queries), BF),
            jax.ShapeDtypeStruct((keys, width), BF),
            jax.ShapeDtypeStruct((keys, width), BF),
        ],
        scratch_shapes=[pltpu.VMEM((keys, 128), F32)] * 2,
        compiler_params=pltpu.CompilerParams(vmem_limit_bytes=56 << 20),
        cost_estimate=pl.CostEstimate(
            flops=40 * queries * keys * width, transcendentals=queries * keys * 2 * pairs, bytes_accessed=2 * width * (5 * queries + 5 * keys)
        ),
        name="attend_back",
    )(k, kt, v, qt, q, gt, g, aug, lse, delta)


def local(
    tokens,
    lengths,
    w_qkv,
    bias_qv,
    w_out,
    bias_out,
    w_up,
    bias_up,
    w_down,
    bias_down,
    gain_attn,
    shift_attn,
    gain_ffn,
    shift_ffn,
    cotangent,
):
    x = tokens[0]
    rows, width = x.shape
    ff = w_up.shape[1]
    me = lax.axis_index("seq")
    other = lax.ppermute(x, "seq", [(0, 1), (1, 0)])

    def gather(value):
        return lax.all_gather(value, "dp", axis=0, tiled=True)

    vectors = (bias_qv, bias_out, bias_up, bias_down, gain_attn, shift_attn, gain_ffn, shift_ffn)
    sizes = [v.shape[0] for v in vectors]
    share = w_qkv.shape[0]
    extra = sum(sizes) // share
    beside = jnp.concatenate(vectors).reshape(share, extra)
    full_qkv = gather(jnp.concatenate([w_qkv, jnp.pad(beside, ((0, 0), (0, 128 - extra)))], axis=1))
    full_vectors = full_qkv[:, 3 * width : 3 * width + extra].reshape(-1, sum(sizes)).astype(F32)
    full_qkv = full_qkv[:, : 3 * width]
    full, start = [], 0
    for size in sizes:
        full.append(full_vectors[:, start : start + size].reshape(-1))
        start += size
    full_bqv, full_bout, full_bup, full_bdown, gain_one, shift_one, gain_two, shift_two = full
    full_wout, full_wup, full_wdown = gather(w_out), gather(w_up), gather(w_down)

    both = jnp.concatenate([x, other], axis=0)
    q = (dot_nn(x, full_qkv[:, :width]) + full_bqv[:width]).astype(BF)
    k = dot_nn(both, full_qkv[:, width : 2 * width]).astype(BF)
    v = (dot_nn(both, full_qkv[:, 2 * width :]) + full_bqv[width:]).astype(BF)
    qt, kt, vt = q.T, k.T, v.T
    slot = jnp.arange(2 * rows)
    slot = jnp.where(slot < rows, me * rows + slot, (1 - me) * rows + slot - rows)
    lane = jnp.arange(128)
    masked = jnp.where(slot < lengths[0], 0.0, MASK)
    aug = jnp.where(lane[None] == 0, masked[:, None], jnp.where(lane[None] < 4, -1.0, 0.0)).astype(BF)
    context_t, lse = attend(k, qt, vt, aug)
    context = context_t.T

    attn_branch = dot_nn(context, full_wout) + full_bout
    resid_one = x.astype(F32) + attn_branch
    hidden_one, first_pull = jax.vjp(layer_norm, resid_one, gain_one, shift_one)
    hidden_low = hidden_one.astype(BF)
    pre_act = dot_nn(hidden_low, full_wup) + full_bup
    activated, gelu_pull = jax.vjp(gelu_exact, pre_act)
    act_low = activated.astype(BF)
    ffn_branch = dot_nn(act_low, full_wdown) + full_bdown
    resid_two = hidden_one + ffn_branch
    output, second_pull = jax.vjp(layer_norm, resid_two, gain_two, shift_two)
    grad_two, grad_gain_two, grad_shift_two = second_pull(cotangent[0].astype(F32))
    grad_branch = grad_two.astype(BF)
    grad_wdown = dot_tn(act_low, grad_branch)
    grad_bdown = column_sum(grad_branch)
    (grad_pre,) = gelu_pull(dot_nt(grad_branch, full_wdown))
    grad_pre_low = grad_pre.astype(BF)
    grad_wup = dot_tn(hidden_low, grad_pre_low)
    grad_bup = column_sum(grad_pre_low)
    grad_hidden = grad_two + dot_nt(grad_pre_low, full_wup)
    grad_one, grad_gain_one, grad_shift_one = first_pull(grad_hidden)
    grad_proj = grad_one.astype(BF)
    grad_wout = dot_tn(context, grad_proj)
    grad_bout = column_sum(grad_proj)
    grad_context = dot_nt(grad_proj, full_wout).astype(BF)
    delta = jnp.sum((grad_context.astype(F32) * context.astype(F32)).reshape(rows, HEADS, HD), axis=-1)
    delta = delta.T.reshape(HEADS // 2, 2, rows)

    def scatter(value):
        part = lax.psum_scatter(value.astype(BF), "dp", scatter_dimension=0, tiled=True)
        return part

    share_wdown = scatter(grad_wdown)
    share_wup = scatter(grad_wup)
    share_wout = scatter(grad_wout)

    dqt, dk, dv = attend_back(k, kt, v, qt, q, grad_context.T, grad_context, aug, lse, delta)
    dq = dqt.T
    partial = dot_nt(jnp.concatenate([dk[rows:], dv[rows:]], axis=1), full_qkv[:, width:])
    partial = lax.ppermute(partial.astype(BF), "seq", [(0, 1), (1, 0)])
    own = jnp.concatenate([dq, dk[:rows], dv[:rows]], axis=1)
    grad_wq = dot_tn(x, dq)
    grad_wk = dot_tn(both, dk)
    grad_wv = dot_tn(both, dv)
    grad_inputs = grad_one + dot_nt(own, full_qkv) + partial.astype(F32)
    grad_bqv = jnp.concatenate([column_sum(dq), column_sum(dv)])

    grads = (grad_bqv, grad_bout, grad_bup, grad_bdown, grad_gain_one, grad_shift_one, grad_gain_two, grad_shift_two)
    packed = jnp.concatenate([v.reshape(-1, size) for v, size in zip(grads, sizes)], axis=1).reshape(width, extra)
    packed = jnp.pad(packed, ((0, 0), (0, 128 - extra)))
    share_qkv = scatter(jnp.concatenate([grad_wq, grad_wk, grad_wv, packed], axis=1))

    def over_seq(value):
        value = value.astype(BF)
        return value.astype(F32) + lax.ppermute(value, "seq", [(0, 1), (1, 0)]).astype(F32)

    share_qkv = over_seq(share_qkv)
    packed = share_qkv[:, 3 * width : 3 * width + extra].reshape(-1)
    out_vectors, start = [], 0
    for size in sizes:
        out_vectors.append(packed[start : start + size])
        start += size
    s_bqv, s_bout, s_bup, s_bdown, s_gain_one, s_shift_one, s_gain_two, s_shift_two = out_vectors
    return (
        output.astype(BF)[None],
        grad_inputs[None],
        share_qkv[:, : 3 * width],
        s_bqv,
        over_seq(share_wout),
        s_bout,
        over_seq(share_wup),
        s_bup,
        over_seq(share_wdown),
        s_bdown,
        s_gain_one,
        s_shift_one,
        s_gain_two,
        s_shift_two,
    )


def solution(mesh):
    act, mat, vec = P("dp", "seq", None), P("dp", None), P("dp")
    in_specs = (act, vec, mat, vec, mat, vec, mat, vec, mat, vec, vec, vec, vec, vec, act)
    out_specs = (act, act, mat, vec, mat, vec, mat, vec, mat, vec, vec, vec, vec, vec)
    return jax.shard_map(local, mesh=mesh, in_specs=in_specs, out_specs=out_specs, check_vma=False)
```

time: 1260 us -> 660 us (0.52)
  matrix products: 411 us -> 118 us
  blocking collectives: 216 us -> 0 us
  other arithmetic: 145 us -> 20.9 us
  Pallas kernels: 0 us -> 115 us
  local copies, waits for them, and re-layouts: 130 us -> 68.1 us
    dot_general x40 -> x17, matrix products: 411 us -> 118 us  [the longest x6 44.1 us: dot_nn(): lax.dot_general(a, b, (((1,), (0,)), ((), ())), preferred_element_type=F32)]
    unnamed x2 -> x0, blocking collectives: 143 us -> none
    pallas_call x0 -> x2, Pallas kernels: none -> 115 us  [the longest x1 73.5 us: attend_back(): pl.pallas_call(functools.partial(attend_back_kernel, chunk), grid=(pairs,...]
    convert_element_type x25 -> x2, other arithmetic: 100 us -> 2.09 us  [the longest x1 1.13 us: local(): jnp.where(lane[None] == 0, masked[:, None], jnp.where(lane[None] < 4, -1....]
    all_gather x4, waiting for transfers between devices: 0.03 us -> 94.7 us  [gather(): return lax.all_gather(value, 'dp', axis=0, tiled=True)]
    all_to_all x3 -> x0, waiting for transfers between devices: 68.1 us -> none  [the longest x1 48.3 us: local(): lax.all_to_all(qkv_low, 'seq', split_axis=2, concat_axis=0, tiled=True)]
    all_to_all x1 -> x0, blocking collectives: 67.8 us -> none  [local(): lax.all_to_all(grad_stack, 'seq', split_axis=0, concat_axis=2, tiled=True)]
    psum x1 -> x0, waiting for transfers between devices: 34.3 us -> none  [local(): lax.psum(share_qkv.astype(jnp.bfloat16), 'seq').astype(jnp.float32)]
  transfers between devices with their start and end apart: 12 -> 14, of which waited for: 6 -> 6; matrix products, arithmetic and copies ran while one was open for 49% -> 20% of each run, Pallas kernels for 0% -> 6%
where the time goes in v1:
time: 660 us; the launch traced here: 653 us
  waiting for transfers between devices  305 us (46%)
  matrix products  118 us (18%)
  Pallas kernels  115 us (17%)
  local copies, waits for them, and re-layouts  68.1 us (10%)
  other arithmetic  20.9 us (3%)
  between operations  15.7 us (2%)
  starting transfers between devices  10.1 us (2%)
    reduce_scatter x4, waiting for transfers between devices, scatter(): lax.psum_scatter(value.astype(BF), 'dp', scatter_dimension=0, tiled=True)  209 us
    all_gather x4, waiting for transfers between devices, gather(): return lax.all_gather(value, 'dp', axis=0, tiled=True)  94.7 us
    pallas_call x1, Pallas kernels, attend_back(): pl.pallas_call(functools.partial(attend_back_kernel, chunk), grid=(pairs,...  73.5 us
    dot_general x6, matrix products, dot_nn(): lax.dot_general(a, b, (((1,), (0,)), ((), ())), preferred_element_type=F32)  44.1 us
    pallas_call x1, Pallas kernels, attend(): pl.pallas_call(functools.partial(attend_kernel, chunk), grid=(pairs, quer...  41.4 us
    dot_general x5, matrix products, dot_nt(): lax.dot_general(a, b, (((1,), (1,)), ((), ())), preferred_element_type=F32)  37.5 us
    dot_general x6, matrix products, dot_tn(): lax.dot_general(a, b, (((0,), (0,)), ((), ())), preferred_element_type=F32)  36.4 us
    unnamed x63, local copies, waits for them, and re-layouts  27.4 us
  transfers between devices with their start and end apart: 14, of which 6 were waited for; matrix products, arithmetic and copies ran while one was open for 20% of the time, Pallas kernels for 6%

profile of v1, /device:TPU:0, one launch (start us, length us, event | category | flops | bytes accessed | tf_op | source)
XLA Modules:
  0.0 652.7 jit_solution(4848541823083675889)
XLA Ops:
  7.2 5.5 concatenate.33
  18.7 2.9 collective-permute-start
  25.2 40.1 %all-gather.5.cloned.1.call-done = bf16[768,2432]{1,0:T(8,128)(2,1)} async-done(((bf16[48,2432]{1,0:T(8,128)(2,1)}), bf16[768,2432]{1,0:T(8,128)(2,1)}) %all-gather.5.cloned.1.call-update) | async-done | bytes 3735568 | tf_op jit(solution)/shard_map/all_gather | solution.py:233
  66.6 6.7 %add_convert_fusion.1.v_ref = bf16[2048,768]{1,0:T(8,128)(2,1)} fusion(f32[768]{0:T(1024)S(1)} %add.167, bf16[768,2432]{1,0:T(8,128)(2,1)} %all-gather.5.cloned.1.call-done, bf16[1024,768]{0,1:T(8,128)(2,1)} %collective-permute-done, bf16[1024,768]{0,1:T(8,128)(2,1)} %bitcast), kind=kOutput, calls=%fused_computation.5 | convolution fusion | flops 2425356288 | bytes 7474176 | tf_op jit(solution)/shard_map/dot_general | solution.py:21
  73.3 4.7 copy.89.vt_ref
  78.0 6.5 %convolution_convert_fusion.2 = bf16[2048,768]{0,1:T(8,128)(2,1)} fusion(bf16[768,2432]{1,0:T(8,128)(2,1)} %all-gather.5.cloned.1.call-done, bf16[1024,768]{0,1:T(8,128)(2,1)} %collective-permute-done, bf16[1024,768]{0,1:T(8,128)(2,1)} %bitcast), kind=kOutput, calls=%fused_computation.22 | convolution fusion | flops 2423783424 | bytes 7471104 | tf_op jit(solution)/shard_map/dot_general | solution.py:21
  84.5 4.8 copy.87.k_ref
  89.4 3.9 add_convert_fusion.3
  96.4 41.4 %attend.1 = (bf16[768,1024]{1,0:T(8,128)(2,1)}, f32[6,2,1024]{2,1,0:T(2,128)}) custom-call(bf16[2048,768]{1,0:T(8,128)(2,1)} %copy.87.k_ref, bf16[768,1024]{1,0:T(8,128)(2,1)} %copy.88.qt_ref, bf16[768,2048]{1,0:T(8,128)(2,1)} %copy.89.vt_ref, bf16[2048,128]{1,0:T(8,128)(2,1)} %select_convert_fusion.aug_ref), custom_call_target="tpu_custom_call" | custom-call | flops 25769803776 | bytes 7864320 | tf_op jit(solution)/shard_map/attend/pallas_call | solution.py:82
  139.6 3.9 fusion.60
  145.6 14.0 %all-gather.9.cloned.1.call-done = bf16[768,3072]{1,0:T(8,128)(2,1)} async-done(((bf16[48,3072]{1,0:T(8,128)(2,1)}), bf16[768,3072]{1,0:T(8,128)(2,1)}) %all-gather.9.cloned.1.call-update) | async-done | bytes 4718608 | tf_op jit(solution)/shard_map/all_gather | solution.py:233
  159.6 13.5 %multiply_convert_fusion = (bf16[1024,3072]{1,0:T(8,128)(2,1)}, f32[1024,3072]{1,0:T(8,128)}) fusion(f32[3072]{0:T(1024)S(1)} %add.182, bf16[768,3072]{1,0:T(8,128)(2,1)} %all-gather.9.cloned.1.call-done, f32[1024,768]{0,1:T(8,128)} %copy-done, f32[768]{0:T(1024)S(1)} %add.179, f32[768]{0:T(1024)S(1)} %mul.154, f32[1024]{0:T(1024)S(1)} %fusion.44, ...), kind=kOutput, calls=%fused_computation.1 | convolution fusion | flops 4854644736 | bytes 26765312 | tf_op jit(solution)/shard_map/dot_general | solution.py:21
  173.1 40.6 %all-gather.11.cloned.1.call-done = bf16[3072,768]{1,0:T(8,128)(2,1)} async-done(((bf16[192,768]{1,0:T(8,128)(2,1)}), bf16[3072,768]{1,0:T(8,128)(2,1)}) %all-gather.11.cloned.1.call-update) | async-done | bytes 4718608 | tf_op jit(solution)/shard_map/all_gather | solution.py:233
  213.8 9.6 %fusion.61 = (f32[1024]{0:T(1024)S(1)}, f32[1024,768]{0,1:T(8,128)S(1)}) fusion(f32[768]{0:T(1024)S(1)} %add.187, bf16[1024,3072]{1,0:T(8,128)(2,1)} %get-tuple-element.102, bf16[3072,768]{1,0:T(8,128)(2,1)} %all-gather.11.cloned.1.call-done, f32[768]{0:T(1024)S(1)} %add.179, f32[768]{0:T(1024)S(1)} %mul.154, f32[1024]{0:T(1024)S(1)} %fusion.44, ...), kind=kOutput, calls=%fused_computation.98 | convolution fusion | flops 4837342208 | bytes 17323008 | tf_op jit(solution)/shard_map/dot_general | solution.py:21
  224.2 2.9 fusion.12
  228.4 15.2 %fusion.62 = (bf16[3072]{0:T(1024)(128)(2,1)S(1)}, bf16[1024,3072]{1,0:T(8,128)(2,1)S(1)}) fusion(bf16[1024,768]{0,1:T(8,128)(2,1)S(1)} %get-tuple-element.74, bf16[3072,768]{1,0:T(8,128)(2,1)S(1)} %bitcast.71, f32[1024,3072]{1,0:T(8,128)} %get-tuple-element.103, f32[3072]{0:T(1024)S(1)} %add.182), kind=kOutput, calls=%fused_computation.99 | convolution fusion | flops 4879021056 | bytes 25184256 | tf_op jit(solution)/shard_map/dot_general | solution.py:25
  243.7 6.6 %multiply_reduce_fusion = (bf16[768]{0:T(1024)(128)(2,1)S(1)}, f32[1024]{0:T(1024)S(1)}, bf16[768]{0:T(1024)(128)(2,1)S(1)}, f32[1024,768]{0,1:T(8,128)S(1)}) fusion(f32[1024,768]{0,1:T(8,128)S(1)} %copy-done.1, f32[1024]{0:T(1024)S(1)} %fusion.44, f32[1024]{0:T(1024)S(1)} %broadcast_multiply_fusion.1, f32[768]{0:T(1024)S(1)} %mul.154, ...), kind=kOutput, calls=%fused_computation.31 | convolution fusion | flops 4845204480 | bytes 22057984 | tf_op jit(solution)/shard_map/dot_general | solution.py:25
  256.2 2.7 convolution_convert_fusion.3.g_ref
  268.2 73.5 %attend_back.1 = (bf16[768,1024]{1,0:T(8,128)(2,1)}, bf16[2048,768]{1,0:T(8,128)(2,1)}, bf16[2048,768]{1,0:T(8,128)(2,1)}) custom-call(bf16[2048,768]{1,0:T(8,128)(2,1)} %copy.87.k_ref, bf16[768,2048]{1,0:T(8,128)(2,1)} %bitcast.64, bf16[2048,768]{1,0:T(8,128)(2,1)} %add_convert_fusion.1.v_ref, bf16[768,1024]{1,0:T(8,128)(2,1)} %copy.88.qt_ref, ...), custom_call_target="tpu_custom_call" | custom-call | flops 64424509440 | bytes 23592960 | tf_op jit(solution)/shard_map/attend_back/pallas_call | solution.py:179
  343.3 4.4 fusion.35
  349.5 4.7 convolution_convert_fusion.5
  354.3 4.8 convolution_convert_fusion.6
  361.2 6.1 copy.121
  368.8 9.8 %convolution_convert_fusion = bf16[3072,768]{1,0:T(8,128)(2,1)} fusion(bf16[1024,3072]{1,0:T(8,128)(2,1)} %get-tuple-element.102, bf16[1024,768]{0,1:T(8,128)(2,1)S(1)} %copy-done.13), kind=kOutput, calls=%fused_computation.6 | convolution fusion | flops 4834197504 | bytes 12582912 | tf_op jit(solution)/shard_map/dot_general | solution.py:29
  380.5 10.0 %convolution_convert_fusion.1 = bf16[768,3072]{1,0:T(8,128)(2,1)} fusion(bf16[1024,3072]{1,0:T(8,128)(2,1)} %copy-done.23, f32[1024,768]{0,1:T(8,128)S(1)} %copy-done.2, f32[768]{0:T(1024)S(1)} %copy-done.22, f32[768]{0:T(1024)S(1)} %mul.154, f32[1024]{0:T(1024)S(1)} %fusion.44, f32[1024]{0:T(1024)S(1)} %broadcast_multiply_fusion.1), kind=kOutput, calls=%fused_computation.7 | convolution fusion | flops 4838129664 | bytes 14170112 | tf_op jit(solution)/shard_map/dot_general | solution.py:29
  392.5 4.1 fusion.55
  396.6 3.7 fusion.23
  407.9 69.3 %reduce-scatter.13.cloned.1.call-done = bf16[48,2432]{1,0:T(8,128)(2,1)} async-done(((bf16[768,2432]{1,0:T(8,128)(2,1)}), bf16[48,2432]{1,0:T(8,128)(2,1)}) %reduce-scatter.13.cloned.1.call-update) | async-done | bytes 233488 | tf_op jit(solution)/shard_map/reduce_scatter | solution.py:291
  478.7 9.3 %add_bitcast_fusion = f32[1,1024,768]{1,2,0:T(8,128)} fusion(bf16[1024,768]{0,1:T(8,128)(2,1)} %collective-permute-done.1, f32[1024,768]{0,1:T(8,128)S(1)} %copy-done.4, bf16[768,2432]{1,0:T(8,128)(2,1)} %all-gather.5.cloned.1.call-done, bf16[1024,768]{1,0:T(8,128)(2,1)} %get-tuple-element.110, bf16[1024,768]{1,0:T(8,128)(2,1)} %get-tuple-element.80, ...), kind=kOutput, calls=%fused_computation.32 | convolution fusion | flops 3641180160 | bytes 16125952 | tf_op jit(solution)/shard_map/dot_general | solution.py:25
  488.0 3.7 copy.113
  493.1 62.8 %reduce-scatter.11.cloned.1.call-done = bf16[192,768]{1,0:T(8,128)(2,1)} async-done(((bf16[3072,768]{1,0:T(8,128)(2,1)}), bf16[192,768]{1,0:T(8,128)(2,1)}) %reduce-scatter.11.cloned.1.call-update) | async-done | bytes 294928 | tf_op jit(solution)/shard_map/reduce_scatter | solution.py:291
  557.4 76.9 %reduce-scatter.9.cloned.1.call-done = bf16[48,3072]{1,0:T(8,128)(2,1)} async-done(((bf16[768,3072]{1,0:T(8,128)(2,1)}), bf16[48,3072]{1,0:T(8,128)(2,1)}) %reduce-scatter.9.cloned.1.call-update) | async-done | bytes 294928 | tf_op jit(solution)/shard_map/reduce_scatter | solution.py:291
  (175 shorter events, 68.3 us)
Async XLA Ops:
  7.2 15.2 %copy-start.7 = (bf16[1,1024,768]{2,1,0:T(8,128)(2,1)S(1)}, bf16[1,1024,768]{2,1,0:T(8,128)(2,1)}, u32[]{:S(2)}) copy-start(bf16[1,1024,768]{2,1,0:T(8,128)(2,1)} %param.29) | copy-start | bytes 4718596
  7.2 58.1 %all-gather.5.cloned.1.call-start = ((), (), s32[]{:S(2)}) async-start(), calls=%async_computation.4 | async-start | bytes 3969024 | tf_op jit(solution)/shard_map/all_gather | solution.py:233
  14.6 125.0 %all-gather.7.cloned.1.call-start = ((), (), s32[]{:S(2)}) async-start(), calls=%async_computation.5 | async-start | bytes 1253376 | tf_op jit(solution)/shard_map/all_gather | solution.py:233
  15.3 144.3 %all-gather.9.cloned.1.call-start = ((), (), s32[]{:S(2)}) async-start(), calls=%async_computation.6 | async-start | bytes 5013504 | tf_op jit(solution)/shard_map/all_gather | solution.py:233
  16.0 197.7 %all-gather.11.cloned.1.call-start = ((), (), s32[]{:S(2)}) async-start(), calls=%async_computation.7 | async-start | bytes 5013504 | tf_op jit(solution)/shard_map/all_gather | solution.py:233
  18.7 47.9 %collective-permute-start = (bf16[1024,768]{0,1:T(8,128)(2,1)}, bf16[1024,768]{0,1:T(8,128)(2,1)}, u32[]{:S(2)}, u32[]{:S(2)}) collective-permute-start(bf16[1024,768]{0,1:T(8,128)(2,1)} %bitcast), channel_id=1, source_target_pairs={{0,16},{16,0},{1,17},{17,1},{2,18},{18,2},{3,19},{19,3},{4,20},{20... | collective-permute-start | bytes 4718600 | tf_op jit(solution)/shard_map/ppermute | solution.py:230
  21.6 385.3 %reduce-scatter.7.cloned.1.call-start = ((), (), s32[]{:S(2)}) async-start(), calls=%async_computation.8 | async-start | bytes 1253376 | tf_op jit(solution)/shard_map/reduce_scatter | solution.py:291
  84.5 4.9 copy-start.10
  96.1 117.7 %copy-start.21 = (f32[768]{0:T(1024)}, f32[768]{0:T(1024)S(1)}, u32[]{:S(2)}) copy-start(f32[768]{0:T(1024)S(1)} %add.179) | copy-start | bytes 9220
  223.4 5.0 slice-start.2
  224.2 4.2 slice-start.3
  227.1 16.5 %slice-start = ((s8[4718592]{0:T(1024)(128)(4,1)}), s8[4194304]{0:T(1024)(128)(4,1)S(1)}, s32[]{:S(2)}) async-start(s8[4718592]{0:T(1024)(128)(4,1)} %bitcast.68), calls=%async_computation.12 | async-start | bytes 8388608
  228.4 15.2 %copy-start.12 = (bf16[1024,768]{0,1:T(8,128)(2,1)}, bf16[1024,768]{0,1:T(8,128)(2,1)S(1)}, u32[]{:S(2)}) copy-start(bf16[1024,768]{0,1:T(8,128)(2,1)S(1)} %get-tuple-element.74) | copy-start | bytes 4718596
  228.4 15.2 %copy-start.1 = (f32[1024,768]{0,1:T(8,128)S(1)}, f32[1024,768]{0,1:T(8,128)}, u32[]{:S(2)}) copy-start(f32[1024,768]{0,1:T(8,128)} %copy-done) | copy-start | bytes 9437188
  228.4 15.2 %slice-start.1 = ((s8[4718592]{0:T(1024)(128)(4,1)}), s8[524288]{0:T(1024)(128)(4,1)S(1)}, s32[]{:S(2)}) async-start(s8[4718592]{0:T(1024)(128)(4,1)} %bitcast.68), calls=%async_computation.13 | async-start | bytes 1048576
  243.6 6.6 %copy-start.23 = (bf16[1024,3072]{1,0:T(8,128)(2,1)}, bf16[1024,3072]{1,0:T(8,128)(2,1)S(1)}, u32[]{:S(2)}) copy-start(bf16[1024,3072]{1,0:T(8,128)(2,1)S(1)} %get-tuple-element.108) | copy-start | bytes 18874372
  343.3 4.6 copy-start.5
  347.8 129.4 %reduce-scatter.13.cloned.1.call-start = ((), (), s32[]{:S(2)}) async-start(), calls=%async_computation.11 | async-start | bytes 3969024 | tf_op jit(solution)/shard_map/reduce_scatter | solution.py:291
  349.5 4.7 copy-start.9
  354.2 4.8 copy-start.14
  367.4 188.5 %reduce-scatter.11.cloned.1.call-start = ((), (), s32[]{:S(2)}) async-start(), calls=%async_computation.10 | async-start | bytes 5013504 | tf_op jit(solution)/shard_map/reduce_scatter | solution.py:291
  378.6 255.7 %reduce-scatter.9.cloned.1.call-start = ((), (), s32[]{:S(2)}) async-start(), calls=%async_computation.9 | async-start | bytes 5013504 | tf_op jit(solution)/shard_map/reduce_scatter | solution.py:291
  392.5 4.1 copy-start.20
  400.3 78.4 %copy-start.4 = (f32[1024,768]{0,1:T(8,128)S(1)}, f32[1024,768]{0,1:T(8,128)}, u32[]{:S(2)}) copy-start(f32[1024,768]{0,1:T(8,128)} %copy-done.3) | copy-start | bytes 9437188
  400.3 78.4 %collective-permute-start.1 = (bf16[1024,768]{0,1:T(8,128)(2,1)}, bf16[1024,768]{0,1:T(8,128)(2,1)}, u32[]{:S(2)}, u32[]{:S(2)}) collective-permute-start(bf16[1024,768]{0,1:T(8,128)(2,1)} %fusion.23), channel_id=1, source_target_pairs={{0,16},{16,0},{1,17},{17,1},{2,18},{18,2},{3,19},{19,3},{4,20},{20... | collective-permute-start | bytes 4718600 | tf_op jit(solution)/shard_map/ppermute | solution.py:301
  407.0 84.7 %collective-permute-start.3 = (bf16[48,768]{1,0:T(8,128)(2,1)}, bf16[48,768]{1,0:T(8,128)(2,1)S(1)}, u32[]{:S(2)}, u32[]{:S(2)}) collective-permute-start(bf16[48,768]{1,0:T(8,128)(2,1)} %reduce-scatter.7.cloned.1.call-done), channel_id=1, source_target_pairs={{0,16},{16,0},{1,17},{17,1},{2,18},{18,2},{3,19},{19,3},{4,20},{20... | collective-permute-start | bytes 221192 | tf_op jit(solution)/shard_map/ppermute | solution.py:316
  477.2 15.5 %collective-permute-start.2 = (bf16[48,2432]{1,0:T(8,128)(2,1)}, bf16[48,2432]{1,0:T(8,128)(2,1)S(1)}, u32[]{:S(2)}, u32[]{:S(2)}) collective-permute-start(bf16[48,2432]{1,0:T(8,128)(2,1)} %reduce-scatter.13.cloned.1.call-done), channel_id=1, source_target_pairs={{0,16},{16,0},{1,17},{17,1},{2,18},{18,2},{3,19},{19,3},{4,20},{20... | collective-permute-start | bytes 700424 | tf_op jit(solution)/shard_map/ppermute | solution.py:316
  488.0 4.4 copy-start.17
  555.8 86.8 %copy-start.15 = (bf16[192,768]{1,0:T(8,128)(2,1)S(1)}, bf16[192,768]{1,0:T(8,128)(2,1)}, u32[]{:S(2)}) copy-start(bf16[192,768]{1,0:T(8,128)(2,1)} %reduce-scatter.11.cloned.1.call-done) | copy-start | bytes 884740
  555.8 86.8 %collective-permute-start.5 = (bf16[192,768]{1,0:T(8,128)(2,1)}, bf16[192,768]{1,0:T(8,128)(2,1)S(1)}, u32[]{:S(2)}, u32[]{:S(2)}) collective-permute-start(bf16[192,768]{1,0:T(8,128)(2,1)} %reduce-scatter.11.cloned.1.call-done), channel_id=1, source_target_pairs={{0,16},{16,0},{1,17},{17,1},{2,18},{18,2},{3,19},{19,3},{4,20},{20... | collective-permute-start | bytes 884744 | tf_op jit(solution)/shard_map/ppermute | solution.py:316
  634.3 9.3 %copy-start.16 = (bf16[48,3072]{1,0:T(8,128)(2,1)S(1)}, bf16[48,3072]{1,0:T(8,128)(2,1)}, u32[]{:S(2)}) copy-start(bf16[48,3072]{1,0:T(8,128)(2,1)} %reduce-scatter.9.cloned.1.call-done) | copy-start | bytes 884740
  634.3 9.3 %collective-permute-start.4 = (bf16[48,3072]{1,0:T(8,128)(2,1)}, bf16[48,3072]{1,0:T(8,128)(2,1)}, u32[]{:S(2)}, u32[]{:S(2)}) collective-permute-start(bf16[48,3072]{1,0:T(8,128)(2,1)} %reduce-scatter.9.cloned.1.call-done), channel_id=1, source_target_pairs={{0,16},{16,0},{1,17},{17,1},{2,18},{18,2},{3,19},{19,3},{4,20},{20... | collective-permute-start | bytes 884744 | tf_op jit(solution)/shard_map/ppermute | solution.py:316
  (10 other events, 19.3 us)
Sparse Core Ops, SparseCore 0:
  14.7 50.5 all-gather.4
  67.6 37.3 all-gather.6
  107.3 52.2 all-gather.8
  161.8 51.9 all-gather.10
  347.9 56.6 reduce-scatter.6
  408.4 68.7 reduce-scatter.12
  481.5 74.2 reduce-scatter.10
  559.7 74.5 reduce-scatter.8

commit v2 on v1

--- a/solution.py
+++ b/solution.py
@@ -206,6 +206,490 @@
     )(k, kt, v, qt, q, gt, g, aug, lse, delta)
 
 
+MESH = pl.DeviceIdType.MESH
+
+
+class Links:
+    def __init__(self, depth, send_sem, recv_sem):
+        index = lax.axis_index("dp")
+        self.depth = depth
+        self.core = index % 2
+        self.near = (index // 2) % 2
+        self.far = index // 4
+        self.seq = lax.axis_index("seq")
+        self.send_sem, self.recv_sem = send_sem, recv_sem
+
+    def peer(self, core=None, near=None, far=None):
+        core = self.core if core is None else core
+        near = self.near if near is None else near
+        far = self.far if far is None else far
+        return {"dp": (far * 2 + near) * 2 + core}
+
+    def to_core(self):
+        return self.peer(core=1 - self.core)
+
+    def to_near(self):
+        return self.peer(near=1 - self.near)
+
+    def to_far(self, k):
+        return self.peer(far=(self.far + k) % self.depth)
+
+    def to_seq(self):
+        return {"seq": 1 - self.seq}
+
+    def all_peers(self):
+        return [self.to_core(), self.to_near(), self.to_seq()] + [self.to_far(k) for k in range(1, self.depth)]
+
+    def barrier(self):
+        semaphore = pltpu.get_barrier_semaphore()
+        peers = self.all_peers()
+        for peer in peers:
+            pl.semaphore_signal(semaphore, inc=1, device_id=peer, device_id_type=MESH)
+        pl.semaphore_wait(semaphore, len(peers))
+
+    def copy(self, src, dst, index, peer):
+        return pltpu.make_async_remote_copy(
+            src_ref=src, dst_ref=dst, send_sem=self.send_sem.at[index], recv_sem=self.recv_sem.at[index], device_id=peer, device_id_type=MESH
+        )
+
+
+class Piece:
+    def __init__(self, links, base, own, from_core, from_near, from_far, from_seq):
+        self.links, self.base = links, base
+        self.own, self.from_core, self.from_near, self.from_far, self.from_seq = own, from_core, from_near, from_far, from_seq
+
+    def near_copy(self):
+        k = self.links
+        return k.copy(self.own.at[:, 1 - k.near], self.from_near, self.base + 1, k.to_near())
+
+    def far_copy(self, distance):
+        k = self.links
+        target = (k.far + distance) % k.depth
+        return k.copy(self.own.at[target, k.near], self.from_far.at[distance - 1], self.base + 2 + distance, k.to_far(distance))
+
+    def seq_copy(self):
+        k = self.links
+        return k.copy(self.own.at[k.far, k.near], self.from_seq, self.base + 2, k.to_seq())
+
+    def send_near(self):
+        k = self.links
+        for z in range(k.depth):
+            total = self.own[z, 1 - k.near].astype(F32) + self.from_core[z, 1 - k.near].astype(F32)
+            self.own[z, 1 - k.near] = total.astype(BF)
+        self.near_copy().start()
+
+    def send_far(self):
+        k = self.links
+        self.near_copy().wait_recv()
+        for z in range(k.depth):
+            total = self.own[z, k.near].astype(F32) + self.from_core[z, k.near].astype(F32) + self.from_near[z].astype(F32)
+            self.own[z, k.near] = total.astype(BF)
+        for distance in range(1, k.depth):
+            self.far_copy(distance).start()
+
+    def send_seq(self):
+        k = self.links
+        total = self.own[k.far, k.near].astype(F32)
+        for distance in range(1, k.depth):
+            self.far_copy(distance).wait_recv()
+            total = total + self.from_far[distance - 1].astype(F32)
+        self.own[k.far, k.near] = total.astype(BF)
+        self.seq_copy().start()
+
+    def result(self):
+        k = self.links
+        self.seq_copy().wait_recv()
+        return self.own[k.far, k.near].astype(F32) + self.from_seq[...].astype(F32)
+
+    def finish(self):
+        self.near_copy().wait_send()
+        for distance in range(1, self.links.depth):
+            self.far_copy(distance).wait_send()
+        self.seq_copy().wait_send()
+
+
+def back_kernel(depth, pairs, early, chunk, *refs):
+    (
+        k_ref,
+        kt_ref,
+        v_ref,
+        qt_ref,
+        q_ref,
+        gt_ref,
+        g_ref,
+        aug_ref,
+        lse_ref,
+        delta_ref,
+        wq_ref,
+        wk_ref,
+        wv_ref,
+        xt_ref,
+        one_ref,
+        sums_ref,
+    ) = refs[:16]
+    n_src = 1 + max(source for source, _, _ in early)
+    sources = refs[16 : 16 + n_src]
+    refs = refs[16 + n_src :]
+    share_qkv = refs[0]
+    shares = refs[1 : 1 + n_src]
+    sums_out, tokens_out = refs[1 + n_src : 3 + n_src]
+    refs = refs[3 + n_src :]
+    stage = [refs[5 * e : 5 * e + 5] for e in range(len(early))]
+    refs = refs[5 * len(early) :]
+    p_full, p_core, p_near, p_far, p_seq, acc, dq_sum, tok_send, tok_recv, dqkv = refs[:10]
+    s_own, s_core, s_near, s_far, s_seq, send_sem, recv_sem, local_sem = refs[10:]
+
+    step = pl.program_id(0)
+    last = 2 * pairs - 1
+    g = step % pairs
+    rows = k_ref.shape[0]
+    queries = qt_ref.shape[1]
+    links = Links(depth, send_sem, recv_sem)
+    span = depth + 2
+    pieces = [Piece(links, e * span, *stage[e]) for e in range(len(early))]
+    pair_base = len(early) * span
+    sums_base = pair_base + pairs * span
+
+    def pair_piece(index):
+        own = p_full.at[index, :, :, links.core]
+        return Piece(links, pair_base + index * span, own, p_core.at[index], p_near.at[index], p_far.at[index], p_seq.at[index])
+
+    def pair_core_copy(index):
+        return links.copy(p_full.at[index, :, :, 1 - links.core], p_core.at[index], pair_base + index * span, links.to_core())
+
+    def early_core_copy(e):
+        source, start, width = early[e]
+        part = sources[source].at[:, :, 1 - links.core, :, pl.ds(start, width)]
+        return links.copy(part, stage[e][1], e * span, links.to_core())
+
+    def early_load(e):
+        source, start, width = early[e]
+        part = sources[source].at[:, :, links.core, :, pl.ds(start, width)]
+        return pltpu.make_async_copy(part, stage[e][0], local_sem.at[e])
+
+    one_copy = pltpu.make_async_copy(one_ref, acc, local_sem.at[len(early)])
+    tokens_copy = links.copy(tok_send, tok_recv, sums_base + span, links.to_seq())
+
+    def early_near(e):
+        early_load(e).wait()
+        early_core_copy(e).wait_recv()
+        pieces[e].send_near()
+
+    def early_done(e):
+        source, start, width = early[e]
+        shares[source][:, start : start + width] = pieces[e].result()
+
+    def pair_near(index):
+        pair_core_copy(index).wait_recv()
+        pair_piece(index).send_near()
+
+    def pair_done(index):
+        value = pair_piece(index).result()
+        for third in range(3):
+            at = pl.multiple_of((third * pairs + index) * 128, 128)
+            share_qkv[:, pl.ds(at, 128)] = value[:, third * 128 : third * 128 + 128]
+
+    @pl.when(step == 0)
+    def _():
+        links.barrier()
+        for e in range(len(early)):
+            early_core_copy(e).start()
+            early_load(e).start()
+        s_own[0] = sums_ref[...]
+
+    def at(moment, when, action, e):
+        @pl.when(moment == when)
+        def _():
+            action(e)
+
+    qt = qt_ref[...]
+    gt = gt_ref[...]
+    q = q_ref[...]
+    grad = g_ref[...]
+    row = lax.broadcasted_iota(jnp.int32, (128, queries), 0)
+    lane = lax.broadcasted_iota(jnp.int32, (queries, 128), 1)
+    query_cols, grad_cols, query_rows, grad_rows = [], [], [], []
+    for h in range(2):
+        down = (row >= HD * h) & (row < HD * h + HD)
+        across = (lane >= HD * h) & (lane < HD * h + HD)
+        tail = three_terms(row, lse_ref[h : h + 1, :] * (1.0 / SCALE)) + jnp.where(row == 0, 1.0, 0.0)
+        query_cols.append(jnp.concatenate([jnp.where(down, qt, 0).astype(BF), tail.astype(BF)], axis=0))
+        tail = three_terms(row, delta_ref[h : h + 1, :])
+        grad_cols.append(jnp.concatenate([jnp.where(down, gt, 0).astype(BF), tail.astype(BF)], axis=0))
+        query_rows.append(jnp.where(across, q, 0).astype(BF))
+        grad_rows.append(jnp.where(across, grad, 0).astype(BF))
+    query_rows = jnp.concatenate(query_rows, axis=0)
+    grad_rows = jnp.concatenate(grad_rows, axis=0)
+    dq = [jnp.zeros((HD, queries), F32)] * 2
+    dv_total = jnp.zeros((1, 128), F32)
+    chunks = rows // chunk
+    for c in range(chunks):
+        part = slice(c * chunk, (c + 1) * chunk)
+        aug = aug_ref[part, :]
+        key = jnp.concatenate([k_ref[part, :], aug], axis=1)
+        value = jnp.concatenate([v_ref[part, :], aug], axis=1)
+        weights, grads = [], []
+        for h in range(2):
+            weight = jnp.exp2(dot_nn(key, query_cols[h]) * EXP2_SCALE)
+            dscore = (weight * dot_nn(value, grad_cols[h])).astype(BF)
+            weights.append(weight.astype(BF))
+            grads.append(dscore)
+            dq[h] = dq[h] + dot_nn(kt_ref[HD * h : HD * h + HD, part], dscore)
+        dv = dot_nn(jnp.concatenate(weights, axis=1), grad_rows)
+        dk = dot_nn(jnp.concatenate(grads, axis=1), query_rows)
+        dqkv[part, 128:256] = (dk * SCALE).astype(BF)
+        dqkv[part, 256:384] = dv.astype(BF)
+        dv_total = dv_total + jnp.sum(dv, axis=0, keepdims=True)
+        if c == chunks // 2 - 1:
+            for e, when in ((0, 0), (2, 2), (4, 5)):
+                at(step, when, early_near, e)
+            for e, when in ((0, 2), (2, 5), (3, 7), (4, 8)):
+                at(step, when, lambda e: pieces[e].send_far(), e)
+            at(step, 4, lambda e: pieces[e].send_seq(), 0)
+            at(step, 8, early_done, 1)
+
+            @pl.when(step >= pairs + 1)
+            def _():
+                pair_near(step - pairs - 1)
+
+            @pl.when(step >= pairs + 2)
+            def _():
+                pair_piece(step - pairs - 2).send_far()
+
+            @pl.when(step >= pairs + 3)
+            def _():
+                pair_piece(step - pairs - 3).send_seq()
+
+            @pl.when(step >= pairs + 4)
+            def _():
+                pair_done(step - pairs - 4)
+
+    dq = jnp.concatenate(dq, axis=0)
+    column = pl.ds(pl.multiple_of(g * 128, 128), 128)
+
+    @pl.when(step < pairs)
+    def _():
+        dq_sum[g] = dq
+        both = jnp.concatenate([wk_ref[...], wv_ref[...]], axis=1)
+        total = dot_nt(dqkv[:, 128:384], both)
+
+        @pl.when(step == 0)
+        def _():
+            acc[...] = total
+
+        @pl.when(step > 0)
+        def _():
+            acc[...] += total
+
+        half = dot_nn(xt_ref[...], dqkv[:, 128:384])
+        p_full[g, :, :, :, :, 128:384] = half.astype(BF).reshape(p_full.shape[1:5] + (256,))
+        s_own[0, 1:2, column] = dv_total
+
+    @pl.when(step == pairs - 1)
+    def _():
+        tok_send[...] = acc[...].astype(BF)
+        tokens_copy.start()
+        one_copy.start()
+
+    @pl.when(step >= pairs)
+    def _():
+        turned = ((dq_sum[g] + dq) * SCALE).T
+        dqkv[:, 0:128] = turned.astype(BF)
+        s_own[0, 0:1, column] = jnp.sum(turned, axis=0, keepdims=True)
+        s_own[0, 1:2, column] += dv_total
+
+        @pl.when(step == pairs)
+        def _():
+            one_copy.wait()
+
+        every = jnp.concatenate([wq_ref[...], wk_ref[...], wv_ref[...]], axis=1)
+        acc[...] += dot_nt(dqkv[...], every)
+        product = dot_nn(xt_ref[...], dqkv[...])
+        shape = p_full.shape[1:5]
+        before = p_full[g, :, :, :, :, 128:384].astype(F32)
+        p_full[g, :, :, :, :, 0:128] = product[:, 0:128].astype(BF).reshape(shape + (128,))
+        p_full[g, :, :, :, :, 128:384] = (product[:, 128:384].reshape(shape + (256,)) + before).astype(BF)
+        pair_core_copy(g).start()
+
+    for e, when in ((1, 0), (3, 3)):
+        at(step, when, early_near, e)
+    at(step, 3, lambda e: pieces[e].send_far(), 1)
+    for e, when in ((1, 5), (2, 7), (3, 9), (4, 9)):
+        at(step, when, lambda e: pieces[e].send_seq(), e)
+    for e, when in ((0, 5), (2, 9)):
+        at(step, when, early_done, e)
+
+    @pl.when(step == last)
+    def _():
+        final = pairs - 1
+        hops = [(s_core, 0, links.to_core()), (s_near, 1, links.to_near())]
+        hops += [(s_far.at[k - 1], 2 + k, links.to_far(k)) for k in range(1, depth)]
+        hops += [(s_seq, 2, links.to_seq())]
+        level = [0, 1] + [2] * (depth - 1) + [3]
+        sums = [links.copy(s_own.at[n], dst, sums_base + index, peer) for n, (dst, index, peer) in zip(level, hops)]
+        sums[0].start()
+        pair_piece(final - 1).send_far()
+        pair_piece(final - 2).send_seq()
+        pair_done(final - 3)
+        pair_near(final)
+        sums[0].wait_recv()
+        s_own[1] = s_own[0] + s_core[...]
+        sums[1].start()
+        tokens_copy.wait_recv()
+        out_copies = []
+        for n in range(4):
+            part = pl.ds(n * (rows // 4), rows // 4)
+            acc[part, :] += tok_recv[part, :].astype(F32)
+            out_copies.append(pltpu.make_async_copy(acc.at[part], tokens_out.at[part], local_sem.at[len(early) + 1 + n]))
+            out_copies[-1].start()
+        pair_piece(final).send_far()
+        sums[1].wait_recv()
+        s_own[2] = s_own[1] + s_near[...]
+        for n in range(2, depth + 1):
+            sums[n].start()
+        pair_piece(final - 1).send_seq()
+        pair_done(final - 2)
+        early_done(3)
+        early_done(4)
+        pair_piece(final).send_seq()
+        total = s_own[2]
+        for n in range(2, depth + 1):
+            sums[n].wait_recv()
+            total = total + s_far[n - 2]
+        s_own[3] = total
+        sums[depth + 1].start()
+        pair_done(final - 1)
+        pair_done(final)
+        sums[depth + 1].wait_recv()
+        sums_out[...] = s_own[3] + s_seq[...]
+        for n in range(4):
+            out_copies[n].wait()
+        for item in sums:
+            item.wait_send()
+        tokens_copy.wait_send()
+        for e in range(len(early)):
+            early_core_copy(e).wait_send()
+            pieces[e].finish()
+        for index in range(pairs):
+            pair_core_copy(index).wait_send()
+            pair_piece(index).finish()
+
+
+EARLY = ((0, 0, 2), (0, 1, 2), (1, 0, 2), (1, 1, 2), (2, 0, 1))
+
+
+def back_reduce(k, kt, v, qt, q, gt, g, aug, lse, delta, full_qkv, xt, grad_one, sums, sources, depth):
+    keys, width = k.shape
+    rows = keys // 2
+    pairs = width // 128
+    chunk = min(256, rows)
+    share = width // (4 * depth)
+    views = [s.reshape(depth, 2, 2, s.shape[0] // (4 * depth), s.shape[1]) for s in sources]
+    early = [(n, part * (views[n].shape[-1] // of), views[n].shape[-1] // of) for n, part, of in EARLY]
+    key_rows = pl.BlockSpec((rows, 128), lambda i: (1 - i // pairs, i % pairs))
+    query_cols = pl.BlockSpec((128, rows), lambda i: (i % pairs, 0))
+    query_rows = pl.BlockSpec((rows, 128), lambda i: (0, i % pairs))
+    stats = pl.BlockSpec((None, 2, rows), lambda i: (i % pairs, 0, 0))
+    whole = pl.BlockSpec(memory_space=pltpu.VMEM)
+    there = pl.BlockSpec(memory_space=pl.ANY)
+    stages = []
+    for n, _, wide in early:
+        high = views[n].shape[3]
+        stages += [
+            pltpu.VMEM((depth, 2, high, wide), BF),
+            pltpu.VMEM((depth, 2, high, wide), BF),
+            pltpu.VMEM((depth, high, wide), BF),
+            pltpu.VMEM((depth - 1, high, wide), BF),
+            pltpu.VMEM((high, wide), BF),
+        ]
+    copies = (len(early) + pairs + 1) * (depth + 2) + 1
+    return pl.pallas_call(
+        functools.partial(back_kernel, depth, pairs, early, chunk),
+        grid=(2 * pairs,),
+        in_specs=[
+            key_rows,
+            pl.BlockSpec((128, rows), lambda i: (i % pairs, 1 - i // pairs)),
+            key_rows,
+            query_cols,
+            query_rows,
+            query_cols,
+            query_rows,
+            pl.BlockSpec((rows, 128), lambda i: (1 - i // pairs, 0)),
+            stats,
+            stats,
+            pl.BlockSpec((width, 128), lambda i: (0, i % pairs)),
+            pl.BlockSpec((width, 128), lambda i: (0, pairs + i % pairs)),
+            pl.BlockSpec((width, 128), lambda i: (0, 2 * pairs + i % pairs)),
+            pl.BlockSpec((width, rows), lambda i: (0, 1 - i // pairs)),
+            there,
+            whole,
+        ]
+        + [there] * len(views),
+        out_specs=[whole] * (2 + len(views)) + [there],
+        out_shape=[jax.ShapeDtypeStruct((share, 3 * width), F32)]
+        + [jax.ShapeDtypeStruct(s.shape[3:], F32) for s in views]
+        + [jax.ShapeDtypeStruct(sums.shape, F32), jax.ShapeDtypeStruct((rows, width), F32)],
+        scratch_shapes=stages
+        + [
+            pltpu.VMEM((pairs, depth, 2, 2, share, 384), BF),
+            pltpu.VMEM((pairs, depth, 2, share, 384), BF),
+            pltpu.VMEM((pairs, depth, share, 384), BF),
+            pltpu.VMEM((pairs, depth - 1, share, 384), BF),
+            pltpu.VMEM((pairs, share, 384), BF),
+            pltpu.VMEM((rows, width), F32),
+            pltpu.VMEM((pairs, 128, rows), F32),
+            pltpu.VMEM((rows, width), BF),
+            pltpu.VMEM((rows, width), BF),
+            pltpu.VMEM((rows, 384), BF),
+            pltpu.VMEM((4,) + sums.shape, F32),
+            pltpu.VMEM(sums.shape, F32),
+            pltpu.VMEM(sums.shape, F32),
+            pltpu.VMEM((depth - 1,) + sums.shape, F32),
+            pltpu.VMEM(sums.shape, F32),
+            pltpu.SemaphoreType.DMA((copies,)),
+            pltpu.SemaphoreType.DMA((copies,)),
+            pltpu.SemaphoreType.DMA((len(early) + 5,)),
+        ],
+        compiler_params=pltpu.CompilerParams(vmem_limit_bytes=58 << 20, collective_id=1, has_side_effects=True),
+        cost_estimate=pl.CostEstimate(
+            flops=40 * rows * keys * width, transcendentals=rows * keys * 2 * pairs, bytes_accessed=2 * width * 20 * rows
+        ),
+        name="back_reduce",
+    )(k, kt, v, qt, q, gt, g, aug, lse, delta, full_qkv, full_qkv, full_qkv, xt, grad_one, sums, *views)
+
+
+def back_plain(k, kt, v, qt, q, grad_context, aug, lse, delta, full_qkv, both, grad_one, grads, sources, sizes):
+    width = k.shape[1]
+    rows = q.shape[0]
+
+    def scatter(value):
+        return lax.psum_scatter(value.astype(BF), "dp", scatter_dimension=0, tiled=True)
+
+    def over_seq(value):
+        value = value.astype(BF)
+        return value.astype(F32) + lax.ppermute(value, "seq", [(0, 1), (1, 0)]).astype(F32)
+
+    share_wout, share_wup, share_wdown = [scatter(s) for s in sources]
+    dqt, dk, dv = attend_back(k, kt, v, qt, q, grad_context.T, grad_context, aug, lse, delta)
+    dq = dqt.T
+    partial = dot_nt(jnp.concatenate([dk[rows:], dv[rows:]], axis=1), full_qkv[:, width:])
+    partial = lax.ppermute(partial.astype(BF), "seq", [(0, 1), (1, 0)])
+    own = jnp.concatenate([dq, dk[:rows], dv[:rows]], axis=1)
+    grad_wq, grad_wk, grad_wv = dot_tn(both[:rows], dq), dot_tn(both, dk), dot_tn(both, dv)
+    grad_inputs = grad_one + dot_nt(own, full_qkv) + partial.astype(F32)
+    grads = (jnp.concatenate([column_sum(dq), column_sum(dv)]),) + tuple(grads)
+    extra = sum(g.shape[0] for g in grads) // width
+    packed = jnp.concatenate([g.reshape(-1, size) for g, size in zip(grads, sizes)], axis=1).reshape(width, extra)
+    packed = jnp.pad(packed, ((0, 0), (0, 128 - extra)))
+    share_qkv = over_seq(scatter(jnp.concatenate([grad_wq, grad_wk, grad_wv, packed], axis=1)))
+    packed = share_qkv[:, 3 * width : 3 * width + extra].reshape(-1)
+    out_vectors, start = [], 0
+    for size in sizes:
+        out_vectors.append(packed[start : start + size])
+        start += size
+    return share_qkv[:, : 3 * width], over_seq(share_wout), over_seq(share_wup), over_seq(share_wdown), out_vectors, grad_inputs
+
+
 def local(
     tokens,
     lengths,
@@ -287,51 +771,36 @@
     delta = jnp.sum((grad_context.astype(F32) * context.astype(F32)).reshape(rows, HEADS, HD), axis=-1)
     delta = delta.T.reshape(HEADS // 2, 2, rows)
 
-    def scatter(value):
-        part = lax.psum_scatter(value.astype(BF), "dp", scatter_dimension=0, tiled=True)
-        return part
-
-    share_wdown = scatter(grad_wdown)
-    share_wup = scatter(grad_wup)
-    share_wout = scatter(grad_wout)
-
-    dqt, dk, dv = attend_back(k, kt, v, qt, q, grad_context.T, grad_context, aug, lse, delta)
-    dq = dqt.T
-    partial = dot_nt(jnp.concatenate([dk[rows:], dv[rows:]], axis=1), full_qkv[:, width:])
-    partial = lax.ppermute(partial.astype(BF), "seq", [(0, 1), (1, 0)])
-    own = jnp.concatenate([dq, dk[:rows], dv[:rows]], axis=1)
-    grad_wq = dot_tn(x, dq)
-    grad_wk = dot_tn(both, dk)
-    grad_wv = dot_tn(both, dv)
-    grad_inputs = grad_one + dot_nt(own, full_qkv) + partial.astype(F32)
-    grad_bqv = jnp.concatenate([column_sum(dq), column_sum(dv)])
-
-    grads = (grad_bqv, grad_bout, grad_bup, grad_bdown, grad_gain_one, grad_shift_one, grad_gain_two, grad_shift_two)
-    packed = jnp.concatenate([v.reshape(-1, size) for v, size in zip(grads, sizes)], axis=1).reshape(width, extra)
-    packed = jnp.pad(packed, ((0, 0), (0, 128 - extra)))
-    share_qkv = scatter(jnp.concatenate([grad_wq, grad_wk, grad_wv, packed], axis=1))
-
-    def over_seq(value):
-        value = value.astype(BF)
-        return value.astype(F32) + lax.ppermute(value, "seq", [(0, 1), (1, 0)]).astype(F32)
-
-    share_qkv = over_seq(share_qkv)
-    packed = share_qkv[:, 3 * width : 3 * width + extra].reshape(-1)
-    out_vectors, start = [], 0
-    for size in sizes:
-        out_vectors.append(packed[start : start + size])
-        start += size
+    parts = lax.axis_size("dp")
+    aligned = parts % 4 == 0 and width % (16 * parts) == 0 and 2 * rows == k.shape[0]
+    grads = (grad_bout, grad_bup, grad_bdown, grad_gain_one, grad_shift_one, grad_gain_two, grad_shift_two)
+    if aligned:
+        sums = jnp.concatenate([g.reshape(-1, width) for g in grads], axis=0)
+        sums = jnp.pad(sums, ((2, 16 - 2 - sums.shape[0]), (0, 0)))
+        sources = (grad_wdown.astype(BF), grad_wup.astype(BF), grad_wout.astype(BF))
+        share_qkv, share_down, share_up, share_out, sums, grad_inputs = back_reduce(
+            k, kt, v, qt, q, grad_context.T, grad_context, aug, lse, delta, full_qkv, jnp.concatenate([x.T, other.T], axis=1), grad_one, sums, sources, parts // 4
+        )
+        out_vectors, start = [], 0
+        sums = sums.reshape(-1)
+        for size in sizes:
+            out_vectors.append(lax.dynamic_slice(sums, (start * parts + lax.axis_index("dp") * size,), (size,)))
+            start += size
+    else:
+        share_qkv, share_out, share_up, share_down, out_vectors, grad_inputs = back_plain(
+            k, kt, v, qt, q, grad_context, aug, lse, delta, full_qkv, both, grad_one, grads, (grad_wout, grad_wup, grad_wdown), sizes
+        )
     s_bqv, s_bout, s_bup, s_bdown, s_gain_one, s_shift_one, s_gain_two, s_shift_two = out_vectors
     return (
         output.astype(BF)[None],
         grad_inputs[None],
-        share_qkv[:, : 3 * width],
+        share_qkv,
         s_bqv,
-        over_seq(share_wout),
+        share_out,
         s_bout,
-        over_seq(share_wup),
+        share_up,
         s_bup,
-        over_seq(share_wdown),
+        share_down,
         s_bdown,
         s_gain_one,
         s_shift_one,

time: 660 us -> 454 us (0.69)
  waiting for transfers between devices: 305 us -> 97 us
  Pallas kernels: 115 us -> 190 us
  matrix products: 118 us -> 76.8 us
  local copies, waits for them, and re-layouts: 68.1 us -> 45.7 us
  starting transfers between devices: 10.1 us -> 3.16 us
    reduce_scatter x4 -> x0, waiting for transfers between devices: 209 us -> none  [scatter(): lax.psum_scatter(value.astype(BF), 'dp', scatter_dimension=0, tiled=True)]
    pallas_call x1, Pallas kernels: 73.5 us -> 148 us  [back_reduce(): pl.pallas_call(functools.partial(back_kernel, depth, pairs, early, chunk)...]
    ppermute x1, waiting for transfers between devices: 0.01 us -> 30.5 us  [local(): other = lax.ppermute(x, 'seq', [(0, 1), (1, 0)])]
    all_gather x4, waiting for transfers between devices: 94.7 us -> 65.1 us  [gather(): return lax.all_gather(value, 'dp', axis=0, tiled=True)]
    dot_general x6 -> x3, matrix products: 36.4 us -> 17.6 us  [dot_tn(): lax.dot_general(a, b, (((0,), (0,)), ((), ())), preferred_element_type=F32)]
    dot_general x5 -> x3, matrix products: 37.5 us -> 21.3 us  [dot_nt(): lax.dot_general(a, b, (((1,), (1,)), ((), ())), preferred_element_type=F32)]
    unnamed x63 -> x45, local copies, waits for them, and re-layouts: 27.4 us -> 12 us
    ppermute x5 -> x0, starting transfers between devices: 6.79 us -> none  [the longest x4 5.36 us: over_seq(): lax.ppermute(value, 'seq', [(0, 1), (1, 0)]).astype(F32)]
  transfers between devices with their start and end apart: 14 -> 5, of which waited for: 6 -> 4; matrix products, arithmetic and copies ran while one was open for 20% -> 12% of each run, Pallas kernels for 6% -> 9%
where the time goes in v2:
time: 454 us; the launch traced here: 446 us
  Pallas kernels  190 us (42%)
  waiting for transfers between devices  97 us (21%)
  matrix products  76.8 us (17%)
  local copies, waits for them, and re-layouts  45.7 us (10%)
  other arithmetic  19 us (4%)
  between operations  15 us (3%)
    pallas_call x1, Pallas kernels, back_reduce(): pl.pallas_call(functools.partial(back_kernel, depth, pairs, early, chunk)...  148 us
    all_gather x4, waiting for transfers between devices, gather(): return lax.all_gather(value, 'dp', axis=0, tiled=True)  65.1 us
    pallas_call x1, Pallas kernels, attend(): pl.pallas_call(functools.partial(attend_kernel, chunk), grid=(pairs, quer...  41.8 us
    dot_general x6, matrix products, dot_nn(): lax.dot_general(a, b, (((1,), (0,)), ((), ())), preferred_element_type=F32)  37.9 us
    ppermute x1, waiting for transfers between devices, local(): other = lax.ppermute(x, 'seq', [(0, 1), (1, 0)])  30.5 us
    dot_general x3, matrix products, dot_nt(): lax.dot_general(a, b, (((1,), (1,)), ((), ())), preferred_element_type=F32)  21.3 us
    dot_general x3, matrix products, dot_tn(): lax.dot_general(a, b, (((0,), (0,)), ((), ())), preferred_element_type=F32)  17.6 us
    unnamed x45, local copies, waits for them, and re-layouts  12 us
  transfers between devices with their start and end apart: 5, of which 4 were waited for; matrix products, arithmetic and copies ran while one was open for 12% of the time, Pallas kernels for 9%

profile of v2, /device:TPU:0, one launch (start us, length us, event | category | flops | bytes accessed | tf_op | source)
XLA Modules:
  0.0 446.2 jit_solution(12556509284839230829)
XLA Ops:
  7.2 5.4 %concatenate.16 = bf16[576]{0:T(1024)(128)(2,1)S(1)} concatenate(bf16[96]{0:T(256)(128)(2,1)} %param.18, bf16[48]{0:T(256)(128)(2,1)} %param.20, bf16[192]{0:T(256)(128)(2,1)} %param.22, bf16[48]{0:T(256)(128)(2,1)} %param.24, bf16[48]{0:T(256)(128)(2,1)} %param.25, bf16[48]{0:T(256)(128)(2,1)} %param.26, bf16[48]{0:T(256)(128)(2,1)} %param.27, bf16[48]{0:T(256)(128)(2,1)} %param.28), dimensions={0} | concatenate | bytes 2304 | tf_op jit(solution)/shard_map/concatenate | solution.py:723
  16.0 3.0 collective-permute-start
  19.7 1.7 convert_reduce_fusion.1
  23.1 30.5 %collective-permute-done = bf16[1024,768]{1,0:T(8,128)(2,1)S(1)} collective-permute-done((bf16[1024,768]{1,0:T(8,128)(2,1)}, bf16[1024,768]{1,0:T(8,128)(2,1)S(1)}, u32[]{:S(2)}, u32[]{:S(2)}) %collective-permute-start) | collective-permute-done | bytes 1572896 | tf_op jit(solution)/shard_map/ppermute | solution.py:714
  54.7 2.1 pad_maximum_fusion.1
  56.8 3.0 copy.55.refs_13_
  59.8 5.4 %all-gather.5.cloned.1.call-done = bf16[768,2432]{1,0:T(8,128)(2,1)} async-done(((bf16[48,2432]{1,0:T(8,128)(2,1)}), bf16[768,2432]{1,0:T(8,128)(2,1)}) %all-gather.5.cloned.1.call-update) | async-done | bytes 3735568 | tf_op jit(solution)/shard_map/all_gather | solution.py:717
  66.7 4.9 %convolution_convert_fusion.2 = bf16[2048,768]{0,1:T(8,128)(2,1)S(1)} fusion(bf16[1024,768]{1,0:T(8,128)(2,1)} %copy-done.7, bf16[1024,768]{1,0:T(8,128)(2,1)} %bitcast.62, bf16[768,2432]{1,0:T(8,128)(2,1)} %all-gather.5.cloned.1.call-done), kind=kOutput, calls=%fused_computation.15 | convolution fusion | flops 2423783424 | bytes 7471104 | tf_op jit(solution)/shard_map/dot_general | solution.py:21
  71.6 3.3 copy.44.k_ref.refs_0_
  74.9 3.1 add_convert_fusion.3
  78.1 1.7 copy.45.qt_ref.refs_3_
  79.8 4.8 %add_convert_fusion.1.refs_2_ = bf16[2048,768]{1,0:T(8,128)(2,1)S(1)} fusion(f32[768]{0:T(1024)S(1)} %add.179, bf16[1024,768]{1,0:T(8,128)(2,1)} %copy-done.7, bf16[1024,768]{1,0:T(8,128)(2,1)} %bitcast.63, bf16[768,2432]{1,0:T(8,128)(2,1)} %all-gather.5.cloned.1.call-done), kind=kOutput, calls=%fused_computation.4 | convolution fusion | flops 2425356288 | bytes 7474176 | tf_op jit(solution)/shard_map/dot_general | solution.py:21
  84.7 3.3 copy.46.vt_ref
  88.3 41.8 %attend.1 = (bf16[768,1024]{1,0:T(8,128)(2,1)}, f32[6,2,1024]{2,1,0:T(2,128)}) custom-call(bf16[2048,768]{1,0:T(8,128)(2,1)} %copy.44.k_ref.refs_0_, bf16[768,1024]{1,0:T(8,128)(2,1)} %copy.45.qt_ref.refs_3_, bf16[768,2048]{1,0:T(8,128)(2,1)} %copy.46.vt_ref, bf16[2048,128]{1,0:T(8,128)(2,1)} %select_convert_fusion.aug_ref.refs_7_), custom_call_target="tpu_custom_call" | custom-call | flops 25769803776 | bytes 7864320 | tf_op jit(solution)/shard_map/attend/pallas_call | solution.py:82
  130.1 2.6 copy.50
  132.6 4.7 %slice.77.refs_10_.refs_11_.refs_12_ = bf16[768,2304]{1,0:T(8,128)(2,1)} slice(bf16[768,2432]{1,0:T(8,128)(2,1)} %all-gather.5.cloned.1.call-done), slice={[0:768], [0:2304]} | slice | bytes 7077888 | tf_op jit(solution)/shard_map/slice | solution.py:726
  137.3 3.9 fusion.29
  141.7 17.8 %all-gather.9.cloned.1.call-done = bf16[768,3072]{1,0:T(8,128)(2,1)} async-done(((bf16[48,3072]{1,0:T(8,128)(2,1)}), bf16[768,3072]{1,0:T(8,128)(2,1)}) %all-gather.9.cloned.1.call-update) | async-done | bytes 4718608 | tf_op jit(solution)/shard_map/all_gather | solution.py:717
  159.5 12.2 %multiply_convert_fusion = (bf16[1024,3072]{1,0:T(8,128)(2,1)}, f32[1024,3072]{1,0:T(8,128)}) fusion(f32[3072]{0:T(1024)S(1)} %add.194, bf16[768,3072]{1,0:T(8,128)(2,1)} %all-gather.9.cloned.1.call-done, f32[1024,768]{1,0:T(8,128)S(1)} %get-tuple-element.59, f32[768]{0:T(1024)S(1)} %add.191, f32[768]{0:T(1024)S(1)} %mul.168, f32[1024]{0:T(1024)S(1)} %fusion.14, ...), kind=kOutput, calls=%fused_computation.2 | convolution fusion | flops 4854644736 | bytes 26765312 | tf_op jit(solution)/shard_map/dot_general | solution.py:21
  171.7 41.9 %all-gather.11.cloned.1.call-done = bf16[3072,768]{1,0:T(8,128)(2,1)} async-done(((bf16[192,768]{1,0:T(8,128)(2,1)}), bf16[3072,768]{1,0:T(8,128)(2,1)}) %all-gather.11.cloned.1.call-update) | async-done | bytes 4718608 | tf_op jit(solution)/shard_map/all_gather | solution.py:717
  213.6 9.0 %fusion.30 = (f32[1024]{0:T(1024)S(1)}, f32[1024,768]{1,0:T(8,128)S(1)}) fusion(f32[768]{0:T(1024)S(1)} %add.199, bf16[1024,3072]{1,0:T(8,128)(2,1)} %get-tuple-element.60, bf16[3072,768]{1,0:T(8,128)(2,1)} %all-gather.11.cloned.1.call-done, f32[768]{0:T(1024)S(1)} %add.191, f32[768]{0:T(1024)S(1)} %mul.168, f32[1024]{0:T(1024)S(1)} %fusion.14, ...), kind=kOutput, calls=%fused_computation.74 | convolution fusion | flops 4837342208 | bytes 17323008 | tf_op jit(solution)/shard_map/dot_general | solution.py:21
  225.3 2.6 fusion.25
  228.7 6.9 %convolution_convert_fusion.1 = bf16[3072,768]{1,0:T(8,128)(2,1)} fusion(bf16[1024,3072]{1,0:T(8,128)(2,1)S(1)} %bitcast.74, bf16[1024,768]{1,0:T(8,128)(2,1)S(1)} %get-tuple-element.36), kind=kOutput, calls=%fused_computation.6 | convolution fusion | flops 4834197504 | bytes 12582912 | tf_op jit(solution)/shard_map/dot_general | solution.py:29
  235.7 13.9 %convert_reduce_fusion = (f32[3072]{0:T(1024)S(1)}, bf16[1024,3072]{1,0:T(8,128)(2,1)S(1)}) fusion(bf16[1024,768]{1,0:T(8,128)(2,1)S(1)} %get-tuple-element.36, bf16[3072,768]{1,0:T(8,128)(2,1)S(1)} %bitcast.69, f32[1024,3072]{1,0:T(8,128)} %get-tuple-element.61, f32[3072]{0:T(1024)S(1)} %add.194), kind=kOutput, calls=%fused_computation | convolution fusion | flops 4882166784 | bytes 25190400 | tf_op jit(solution)/shard_map/dot_general | solution.py:25
  249.6 8.2 %convolution_convert_fusion = bf16[768,3072]{1,0:T(8,128)(2,1)} fusion(bf16[1024,3072]{1,0:T(8,128)(2,1)S(1)} %get-tuple-element.66, f32[1024,768]{1,0:T(8,128)S(1)} %get-tuple-element.59, f32[768]{0:T(1024)S(1)} %add.191, f32[768]{0:T(1024)S(1)} %mul.168, f32[1024]{0:T(1024)S(1)} %fusion.14, f32[1024]{0:T(1024)S(1)} %broadcast_multiply_fusion.1), kind=kOutput, calls=%fused_computation.5 | convolution fusion | flops 4838129664 | bytes 14170112 | tf_op jit(solution)/shard_map/dot_general | solution.py:29
  257.8 6.0 %multiply_reduce_fusion = (f32[768]{0:T(1024)S(1)}, f32[1024]{0:T(1024)S(1)}, f32[768]{0:T(1024)S(1)}, f32[1024,768]{1,0:T(8,128)S(1)}) fusion(f32[1024,768]{1,0:T(8,128)S(1)} %get-tuple-element.59, f32[1024]{0:T(1024)S(1)} %fusion.14, f32[1024]{0:T(1024)S(1)} %broadcast_multiply_fusion.1, f32[768]{0:T(1024)S(1)} %mul.168, ...), kind=kOutput, calls=%fused_computation.21 | convolution fusion | flops 4839699456 | bytes 20472832 | tf_op jit(solution)/shard_map/dot_general | solution.py:25
  267.0 2.4 convolution_convert_fusion.4
  273.7 2.2 bitcast_multiply_fusion
  275.9 2.5 copy.51
  278.4 2.3 reduce_sum.154
  282.1 147.8 %back_reduce.1 = (f32[48,2304]{1,0:T(8,128)}, f32[192,768]{1,0:T(8,128)}, f32[48,3072]{1,0:T(8,128)}, f32[48,768]{1,0:T(8,128)}, f32[16,768]{1,0:T(8,128)}, /*index=5*/f32[1024,768]{1,0:T(8,128)}) custom-call(bf16[2048,768]{1,0:T(8,128)(2,1)} %copy.44.k_ref.refs_0_, bf16[768,2048]{1,0:T(8,128)(2,1)} %bitcast.56, bf16[2048,768]{1,0:T(8,128)(2,1)} %copy-done.3, ...), custom_call_target="tpu_custom_call" | custom-call | flops 64424509440 | bytes 31457280 | tf_op jit(solution)/shard_map/back_reduce/pallas_call | solution.py:606
  432.6 3.9 copy.67
  (106 shorter events, 26.6 us)
Async XLA Ops:
  7.2 57.9 %all-gather.5.cloned.1.call-start = ((), (), s32[]{:S(2)}) async-start(), calls=%async_computation | async-start | bytes 3969024 | tf_op jit(solution)/shard_map/all_gather | solution.py:717
  14.4 122.9 %all-gather.7.cloned.1.call-start = ((), (), s32[]{:S(2)}) async-start(), calls=%async_computation.1 | async-start | bytes 1253376 | tf_op jit(solution)/shard_map/all_gather | solution.py:717
  15.2 144.3 %all-gather.9.cloned.1.call-start = ((), (), s32[]{:S(2)}) async-start(), calls=%async_computation.2 | async-start | bytes 5013504 | tf_op jit(solution)/shard_map/all_gather | solution.py:717
  15.9 197.7 %all-gather.11.cloned.1.call-start = ((), (), s32[]{:S(2)}) async-start(), calls=%async_computation.3 | async-start | bytes 5013504 | tf_op jit(solution)/shard_map/all_gather | solution.py:717
  16.0 37.6 %collective-permute-start = (bf16[1024,768]{1,0:T(8,128)(2,1)}, bf16[1024,768]{1,0:T(8,128)(2,1)S(1)}, u32[]{:S(2)}, u32[]{:S(2)}) collective-permute-start(bf16[1024,768]{1,0:T(8,128)(2,1)} %bitcast.60), channel_id=1, source_target_pairs={{0,16},{16,0},{1,17},{17,1},{2,18},{18,2},{3,19},{19,3},{4,20},{20... | collective-permute-start | bytes 4718600 | tf_op jit(solution)/shard_map/ppermute | solution.py:714
  53.6 1.1 copy-start.7
  71.5 3.3 copy-start.2
  78.1 1.7 copy-start.5
  84.7 3.3 copy-start.3
  222.6 1.4 copy-start
  225.3 3.0 slice-start.4
  225.3 3.4 slice-start.5
  227.9 7.7 %slice-start.2 = ((s8[4718592]{0:T(1024)(128)(4,1)}), s8[4194304]{0:T(1024)(128)(4,1)S(1)}, s32[]{:S(2)}) async-start(s8[4718592]{0:T(1024)(128)(4,1)} %bitcast.68), calls=%async_computation.6 | async-start | bytes 8388608
  228.7 6.9 %slice-start.3 = ((s8[4718592]{0:T(1024)(128)(4,1)}), s8[524288]{0:T(1024)(128)(4,1)S(1)}, s32[]{:S(2)}) async-start(s8[4718592]{0:T(1024)(128)(4,1)} %bitcast.68), calls=%async_computation.7 | async-start | bytes 1048576
  228.7 29.1 %slice-start = ((s8[4718592]{0:T(1024)(128)(4,1)}), s8[4194304]{0:T(1024)(128)(4,1)S(1)}, s32[]{:S(2)}) async-start(s8[4718592]{0:T(1024)(128)(4,1)} %bitcast.66), calls=%async_computation.4 | async-start | bytes 8388608
  235.7 22.1 %slice-start.1 = ((s8[4718592]{0:T(1024)(128)(4,1)}), s8[524288]{0:T(1024)(128)(4,1)S(1)}, s32[]{:S(2)}) async-start(s8[4718592]{0:T(1024)(128)(4,1)} %bitcast.66), calls=%async_computation.5 | async-start | bytes 1048576
  265.3 1.7 copy-start.6
  265.7 3.7 copy-start.4
  267.0 2.4 copy-start.13
  270.8 1.2 copy-start.1
  278.4 3.0 copy-start.12
  432.6 3.9 copy-start.10
  432.6 4.7 %copy-start.11 = (f32[48,768]{1,0:T(8,128)S(1)}, f32[48,768]{1,0:T(8,128)}, u32[]{:S(2)}) copy-start(f32[48,768]{1,0:T(8,128)} %get-tuple-element.85) | copy-start | bytes 442372
  432.6 5.3 %copy-start.9 = (f32[48,3072]{1,0:T(8,128)S(1)}, f32[48,3072]{1,0:T(8,128)}, u32[]{:S(2)}) copy-start(f32[48,3072]{1,0:T(8,128)} %get-tuple-element.87) | copy-start | bytes 1769476
  432.6 6.1 %copy-start.8 = (f32[192,768]{1,0:T(8,128)S(1)}, f32[192,768]{1,0:T(8,128)}, u32[]{:S(2)}) copy-start(f32[192,768]{1,0:T(8,128)} %get-tuple-element.89) | copy-start | bytes 1769476
Sparse Core Ops, SparseCore 0:
  14.6 50.5 all-gather.4
  67.4 37.3 all-gather.6
  107.1 52.3 all-gather.8
  161.6 51.9 all-gather.10
